TPU v7x, 32 devices: a whole 2x2x4 slice. The times are simulated.
32 devices in a mesh: ctx: 8 (over z, x), tp: 4 (over y, core).
Axes of the slice: x: 2, y: 2, z: 4, core: 2. Of those that a mesh axis runs over, the one named last changes fastest.
Arguments:
- layer_input: bfloat16 [2048, 2048], P('ctx', 'tp'), may hold values from -6 to 6
- norm_gain: bfloat16 [2048], P('tp'), may hold values from 0.5 to 1.5
- norm_shift: bfloat16 [2048], P('tp'), may hold values from -3 to 3
- w_qkv: bfloat16 [2048, 3, 2048], P('ctx', None, 'tp'), may hold values from -1 to 1
- b_qkv: float32 [3, 2048], P(None, 'tp'), may hold values from -3 to 3
- w_out: bfloat16 [2048, 2048], P('tp', 'ctx'), may hold values from -0.125 to 0.125
- b_out: float32 [2048], P('tp'), may hold values from -3 to 3
- w_fc1: bfloat16 [2048, 8192], P('ctx', 'tp'), may hold values from -0.125 to 0.125
- b_fc1: float32 [8192], P('tp'), may hold values from -3 to 3
- w_fc2: bfloat16 [8192, 2048], P('tp', 'ctx'), may hold values from -0.0625 to 0.0625
- b_fc2: float32 [2048], P('tp'), may hold values from -3 to 3
- grad_output: bfloat16 [2048, 2048], P('ctx', 'tp'), may hold values from -6 to 6
- placement: int32 [16], replicated, may hold values from 0 to 15, as said below
- position_ids: int32 [2048], P('ctx'), may hold values from 0 to 4095
Outputs:
- layer_output: float32 [2048, 2048], P('ctx', 'tp')
- grad_input: float32 [2048, 2048], P('ctx', 'tp')
- grad_norm_gain: float32 [2048], P('tp')
- grad_norm_shift: float32 [2048], P('tp')
- grad_w_qkv: float32 [2048, 3, 2048], P('ctx', None, 'tp')
- grad_b_qkv: float32 [3, 2048], P(None, 'tp')
- grad_w_out: float32 [2048, 2048], P('tp', 'ctx')
- grad_b_out: float32 [2048], P('tp')
- grad_w_fc1: float32 [2048, 8192], P('ctx', 'tp')
- grad_b_fc1: float32 [8192], P('tp')
- grad_w_fc2: float32 [8192, 2048], P('tp', 'ctx')
- grad_b_fc2: float32 [2048], P('tp')
Inputs may be any that keep to these rules, and one draw needn't show every extreme that they name: `placement`: stored blocks 2 c and 2 c + 1 sit on index c of ctx; entry 2 c is some block a and entry 2 c + 1 is 15 - a, with the values a over all c a permutation of 0 to 7.
All inputs are finite; a program needn't handle non-finite values.
Results may differ from a plain program's by a relative error of at most 0.019.
Values may be sent and summed in bfloat16 or wider, within the bound.
No kernel may reach another device: no remote copies, remote signals or barrier semaphores. Data moves between devices by JAX's collectives and lax.ppermute only.
A program may use at most 192 MiB of HBM per device.

v0:
```python
import functools
import math

import jax
import jax.numpy as jnp
from jax import lax
from jax.experimental import pallas as pl
from jax.experimental.pallas import tpu as pltpu
from jax.sharding import Mesh, PartitionSpec as P


D = 2048
HD = 64
ROT = 32
BLK = 128
HALF = BLK // 2
LO = 8
UNIT = 1024
STEP = 256

epsilon = 1e-05
cubic_coef = 0.044715
inner_coef = math.sqrt(2.0 / math.pi)
neg_large = -1e30
BF = jnp.bfloat16
F32 = jnp.float32
LOX = ("zh", "zl", "x")
CTX = ("hi",) + LOX
TP = ("y", "k")


def swap(values, axis):
    return lax.ppermute(values, axis, [(0, 1), (1, 0)])


def spread(pieces):
    return lax.all_to_all(pieces, LOX, 0, 0, tiled=True)


def gather_pieces(unit):
    unit = unit.reshape(2, HALF, UNIT)
    pair = jnp.stack([unit, swap(unit, "zh")])
    quad = jnp.concatenate([pair, swap(pair, "zl")])
    first, second = quad[:, 0], quad[:, 1]
    firsts = jnp.stack([first, swap(first, "x")])
    seconds = jnp.stack([second, swap(second, "y")])
    firsts_y = swap(firsts, "y")
    return firsts, firsts_y, seconds, swap(seconds, "x")


def scatter_pieces(a_own, a_other, b_near, b_far):
    def add(left, right):
        return left.astype(F32) + right.astype(F32)

    a_own = add(a_own, swap(a_other, "y")).astype(BF)
    b_near = add(b_near, swap(b_far, "x")).astype(BF)
    a_own = add(a_own[:4], swap(a_own[4:], "x")).astype(BF)
    b_near = add(b_near[:, 0], swap(b_near[:, 1], "y")).astype(BF)
    both = jnp.stack([a_own, b_near], axis=1)
    both = add(both[:2], swap(both[2:], "zl")).astype(BF)
    return add(both[0], swap(both[1], "zh")).reshape(BLK, UNIT)


def full_spec(count):
    return [pl.BlockSpec(memory_space=pltpu.VMEM) for _ in range(count)]


def dot(left, right, left_dim, right_dim):
    return lax.dot_general(
        left, right, (((left_dim,), (right_dim,)), ((), ())), preferred_element_type=F32
    )


def cost(flops, size):
    return pl.CostEstimate(flops=flops, bytes_accessed=size, transcendentals=0)


def rows_spec(columns, step=STEP):
    return pl.BlockSpec((step, columns), lambda i: (i, 0))


def fixed_spec(*shape):
    return pl.BlockSpec(shape, lambda i: (0,) * len(shape))


def scalar_spec():
    return pl.BlockSpec(memory_space=pltpu.SMEM)


def piece_specs():
    near = pl.BlockSpec((1, 2, HALF, UNIT), lambda i: (i // 2, i % 2, 0, 0))
    both = pl.BlockSpec((2, 2, HALF, UNIT), lambda i: (0, i % 2, 0, 0))
    return [near, near, both, both]


def piece_rows(step, firsts, firsts_y, seconds, seconds_x):
    later = jnp.where(step < 2, seconds[...], seconds_x[...])
    sides = []
    for side, first in enumerate((firsts, firsts_y)):
        parts = []
        for s in range(2):
            parts += [first[0, s], later[side, s]]
        sides.append(jnp.concatenate(parts, axis=0))
    return sides


def sides_of(place):
    y = place[0]
    return [
        pl.ds(pl.multiple_of(y * UNIT, UNIT), UNIT),
        pl.ds(pl.multiple_of((1 - y) * UNIT, UNIT), UNIT),
    ]


def pack_kernel(weight, out):
    for c in range(LO):
        columns = slice(c * HD, (c + 1) * HD)
        for j in range(3):
            out[c, j] = jnp.concatenate(
                [weight[j, :BLK, columns], weight[j, BLK:, columns]], axis=1
            )


def pack_heads(weight):
    return pl.pallas_call(
        pack_kernel,
        out_shape=jax.ShapeDtypeStruct((LO, 3, BLK, BLK), BF),
        in_specs=full_spec(1),
        out_specs=full_spec(1)[0],
        cost_estimate=cost(0, 1600000),
        name="pack",
    )(weight)


def join_kernel(own, other, out):
    for c in range(LO):
        for u in range(2):
            columns = slice(u * HD, (u + 1) * HD)
            rows = pl.ds(c * 2 * BLK + u * BLK, BLK)
            for j in range(3):
                out[rows, j * BLK : (j + 1) * BLK] = jnp.concatenate(
                    [own[c, j, :, columns], other[c, j, :, columns]], axis=1
                )


def join_heads(own, other):
    return pl.pallas_call(
        join_kernel,
        out_shape=jax.ShapeDtypeStruct((D, 3 * BLK), BF),
        in_specs=full_spec(2),
        out_specs=full_spec(1)[0],
        cost_estimate=cost(0, 3200000),
        name="join",
    )(own, other)


def pack_grad_kernel(fc1_own, fc1_other, own, other, out):
    for c in range(LO):
        rows = pl.ds(c * 2 * BLK, 2 * BLK)
        out[c, : 2 * BLK] = (fc1_own[rows, :] + fc1_other[rows, :].astype(F32)).astype(BF)
        tiles = []
        for j in range(3):
            columns = slice(j * HD, (j + 1) * HD)
            parts = []
            for u in range(2):
                rows = pl.ds(c * 2 * BLK + u * BLK, BLK)
                parts.append(own[rows, columns] + other[rows, columns].astype(F32))
            tiles.append(jnp.concatenate(parts, axis=1).astype(BF))
        out[c, 2 * BLK : 3 * BLK] = jnp.concatenate(tiles[:2], axis=1)
        out[c, 3 * BLK :] = jnp.concatenate([tiles[2][:HALF], tiles[2][HALF:]], axis=1)


def pack_grads(fc1_own, fc1_other, own, other):
    return pl.pallas_call(
        pack_grad_kernel,
        out_shape=jax.ShapeDtypeStruct((LO, 3 * BLK + HALF, 2 * BLK), BF),
        in_specs=full_spec(4),
        out_specs=full_spec(1)[0],
        cost_estimate=cost(0, 9000000),
        name="pack_grad",
    )(fc1_own, fc1_other, own, other)


def home_kernel(pieces, fc1, qkv):
    for c in range(LO):
        fc1[:, c * 256 : (c + 1) * 256] = pieces[c, : 2 * BLK].astype(F32)
    for c in range(0, LO, 2):
        for j in range(3):
            tiles = []
            for d in range(2):
                if j < 2:
                    tiles.append(pieces[c + d, 2 * BLK : 3 * BLK, j * BLK : (j + 1) * BLK])
                else:
                    tiles.append(
                        jnp.concatenate(
                            [pieces[c + d, 3 * BLK :, :BLK], pieces[c + d, 3 * BLK :, BLK:]],
                            axis=0,
                        )
                    )
            for u in range(2):
                columns = slice(u * HD, (u + 1) * HD)
                qkv[j, u * BLK : (u + 1) * BLK, c * HD : (c + 2) * HD] = jnp.concatenate(
                    [tile[:, columns] for tile in tiles], axis=1
                ).astype(F32)


def home_grads(pieces):
    return pl.pallas_call(
        home_kernel,
        out_shape=(
            jax.ShapeDtypeStruct((2 * BLK, LO * 256), F32),
            jax.ShapeDtypeStruct((3, 2 * BLK, LO * HD), F32),
        ),
        in_specs=full_spec(1),
        out_specs=tuple(full_spec(2)),
        cost_estimate=cost(0, 6000000),
        name="home",
    )(pieces)


def turn(values, cosine, sine_a, sine_b):
    return (
        values * cosine
        + pltpu.roll(values, 128 - ROT // 2, 1) * sine_a
        + pltpu.roll(values, ROT // 2, 1) * sine_b
    )


def sort_in(table, own, other, target, blocks):
    core = table[0]
    for i in range(blocks):
        place = table[1 + i]
        rows = pl.ds(i * HALF, HALF)
        target[pl.ds(pl.multiple_of(place * BLK + core * HALF, HALF), HALF), :] = own[rows, :]
        target[pl.ds(pl.multiple_of(place * BLK + (1 - core) * HALF, HALF), HALF), :] = other[
            rows, :
        ]


def two_heads(tile):
    lane = lax.broadcasted_iota(jnp.int32, tile.shape, 1)
    zero = jnp.zeros_like(tile)
    return jnp.concatenate(
        [jnp.where(lane < HD, tile, zero), jnp.where(lane < HD, zero, tile)], axis=0
    )


def one_tile(pair):
    rows = pair.shape[0] // 2
    lane = lax.broadcasted_iota(jnp.int32, (rows, pair.shape[1]), 1)
    return jnp.where(lane < HD, pair[:rows], pair[rows:])


def attend_kernel(
    tiles, blocks, table, q, k_own, v_own, k_other, v_other, out, log_out, qs, ks, vs, os, ls
):
    core = table[0]
    sort_in(table, k_own, k_other, ks, blocks)
    sort_in(table, v_own, v_other, vs, blocks)
    for i in range(2 * LO):
        place = table[1 + blocks + i]
        qs[pl.ds(pl.multiple_of(place * HALF, HALF), HALF), :] = q[pl.ds(i * HALF, HALF), :]
    scale = 1.0 / math.sqrt(HD)
    full = len(tiles) > 0 and tiles[0] == tiles[-1] and len(tiles) > 1
    row = lax.broadcasted_iota(jnp.int32, (2 * BLK, 4 * BLK), 0) % BLK
    col = lax.broadcasted_iota(jnp.int32, (2 * BLK, 4 * BLK), 1)
    edge = col - (row // HALF) * BLK - core * HALF - row % HALF

    def tile(m, extent):
        pair = two_heads(qs[pl.ds(pl.multiple_of(m * BLK, BLK), BLK), :])
        scores = dot(pair, ks[pl.ds(0, extent), :], 1, 1) * scale
        if full:
            wide_col = lax.broadcasted_iota(jnp.int32, scores.shape, 1)
            wide_row = lax.broadcasted_iota(jnp.int32, scores.shape, 0) % BLK
            begin = jnp.where(
                wide_row < HALF,
                table[1 + blocks + 2 * LO + 2 * m],
                table[2 + blocks + 2 * LO + 2 * m],
            )
            allowed = wide_col <= begin * BLK + core * HALF + wide_row % HALF
            scores = jnp.where(allowed, scores, neg_large)
        else:
            last = scores[:, extent - 4 * BLK :]
            last = jnp.where(edge <= (m % 2) * (2 * BLK), last, neg_large)
            if extent > 4 * BLK:
                scores = jnp.concatenate([scores[:, : extent - 4 * BLK], last], axis=1)
            else:
                scores = last
        top = jnp.max(scores, axis=-1, keepdims=True)
        weights = jnp.exp(scores - top)
        total = jnp.sum(weights, axis=-1, keepdims=True)
        probs = (weights * (1.0 / total)).astype(BF)
        mixed = dot(probs, vs[pl.ds(0, extent), :], 1, 0)
        os[pl.ds(pl.multiple_of(m * BLK, BLK), BLK), :] = one_tile(mixed)
        ls[pl.ds(pl.multiple_of(m * BLK, BLK), BLK), :] = one_tile(
            jnp.broadcast_to(top + jnp.log(total), (2 * BLK, 128))
        )

    if full:
        lax.fori_loop(0, len(tiles), lambda m, carry: (tile(m, tiles[0]), carry)[1], 0)
    else:
        for m in range(0, len(tiles), 2):
            lax.fori_loop(m, m + 2, lambda i, carry: (tile(i, tiles[m]), carry)[1], 0)
    for i in range(2 * LO):
        place = table[1 + blocks + i]
        rows = pl.ds(pl.multiple_of(place * HALF, HALF), HALF)
        out[pl.ds(i * HALF, HALF), :] = os[rows, :].astype(BF)
        log_out[pl.ds(i * HALF, HALF), :] = ls[rows, :]


def attend(tiles, blocks, table, q, k_own, v_own, k_other, v_other):
    tokens = q.shape[0]
    keys = blocks * BLK
    return pl.pallas_call(
        functools.partial(attend_kernel, tiles, blocks),
        out_shape=(
            jax.ShapeDtypeStruct((tokens, 128), BF),
            jax.ShapeDtypeStruct((tokens, 128), F32),
        ),
        in_specs=[pl.BlockSpec(memory_space=pltpu.SMEM)] + full_spec(5),
        out_specs=tuple(full_spec(2)),
        scratch_shapes=[
            pltpu.VMEM((tokens, 128), BF),
            pltpu.VMEM((keys, 128), BF),
            pltpu.VMEM((keys, 128), BF),
            pltpu.VMEM((tokens, 128), F32),
            pltpu.VMEM((tokens, 128), F32),
        ],
        cost_estimate=pl.CostEstimate(
            flops=8 * 256 * 128 * sum(tiles),
            bytes_accessed=2000000,
            transcendentals=256 * sum(tiles),
        ),
        name="attend",
    )(table, q, k_own, v_own, k_other, v_other)


def attend_back_kernel(
    tiles,
    blocks,
    table,
    q,
    k_own,
    v_own,
    k_other,
    v_other,
    cot,
    att,
    log_in,
    dq,
    dk_own,
    dv_own,
    sent,
    qs,
    ks,
    vs,
    cs,
    ps,
    ls,
    dqs,
    dks,
    dvs,
):
    core = table[0]
    sort_in(table, k_own, k_other, ks, blocks)
    sort_in(table, v_own, v_other, vs, blocks)
    for i in range(2 * LO):
        place = table[1 + blocks + i]
        rows = pl.ds(i * HALF, HALF)
        target = pl.ds(pl.multiple_of(place * HALF, HALF), HALF)
        qs[target, :] = q[rows, :]
        cs[target, :] = cot[rows, :]
        ps[target, :] = cot[rows, :].astype(F32) * att[rows, :].astype(F32)
        ls[target, :] = log_in[rows, :]
    dks[...] = jnp.zeros_like(dks)
    dvs[...] = jnp.zeros_like(dvs)
    scale = 1.0 / math.sqrt(HD)
    full = len(tiles) > 0 and tiles[0] == tiles[-1] and len(tiles) > 1
    col = lax.broadcasted_iota(jnp.int32, (4 * BLK, 2 * BLK), 1) % BLK
    row = lax.broadcasted_iota(jnp.int32, (4 * BLK, 2 * BLK), 0)
    edge = row - (col // HALF) * BLK - core * HALF - col % HALF

    def tile(m, extent):
        rows = pl.ds(pl.multiple_of(m * BLK, BLK), BLK)
        span = pl.ds(0, extent)
        pair = two_heads(qs[rows, :])
        cot_pair = two_heads(cs[rows, :])
        logs = jnp.transpose(ls[rows, :])
        log_row = jnp.concatenate([logs[0:1], logs[HD : HD + 1]], axis=1)
        products = jnp.transpose(ps[rows, :])
        delta = jnp.concatenate(
            [
                jnp.sum(products[:HD], axis=0, keepdims=True),
                jnp.sum(products[HD:], axis=0, keepdims=True),
            ],
            axis=1,
        )
        scores = dot(ks[span, :], pair, 1, 1) * scale
        probs = jnp.exp(scores - log_row)
        if full:
            wide_row = lax.broadcasted_iota(jnp.int32, scores.shape, 0)
            wide_col = lax.broadcasted_iota(jnp.int32, scores.shape, 1) % BLK
            begin = jnp.where(
                wide_col < HALF,
                table[1 + blocks + 2 * LO + 2 * m],
                table[2 + blocks + 2 * LO + 2 * m],
            )
            allowed = wide_row <= begin * BLK + core * HALF + wide_col % HALF
            probs = jnp.where(allowed, probs, 0.0)
        else:
            last = jnp.where(edge <= (m % 2) * (2 * BLK), probs[extent - 4 * BLK :], 0.0)
            if extent > 4 * BLK:
                probs = jnp.concatenate([probs[: extent - 4 * BLK], last], axis=0)
            else:
                probs = last
        grad_probs = dot(vs[span, :], cot_pair, 1, 1)
        grad_scores = (probs * (grad_probs - delta)).astype(BF)
        dvs[span, :] += dot(probs.astype(BF), cot_pair, 1, 0)
        dks[span, :] += dot(grad_scores, pair, 1, 0)
        dqs[rows, :] = one_tile(dot(grad_scores, ks[span, :], 0, 0)) * scale

    if full:
        lax.fori_loop(0, len(tiles), lambda m, carry: (tile(m, tiles[0]), carry)[1], 0)
    else:
        for m in range(0, len(tiles), 2):
            lax.fori_loop(m, m + 2, lambda i, carry: (tile(i, tiles[m]), carry)[1], 0)
    for i in range(2 * LO):
        place = table[1 + blocks + i]
        dq[pl.ds(i * HALF, HALF), :] = dqs[
            pl.ds(pl.multiple_of(place * HALF, HALF), HALF), :
        ]
    for i in range(blocks):
        place = table[1 + i]
        rows = pl.ds(i * HALF, HALF)
        own = pl.ds(pl.multiple_of(place * BLK + core * HALF, HALF), HALF)
        other = pl.ds(pl.multiple_of(place * BLK + (1 - core) * HALF, HALF), HALF)
        dk_own[rows, :] = dks[own, :] * scale
        dv_own[rows, :] = dvs[own, :]
        sent[0, rows, :] = pltpu.roll(dks[other, :] * scale, HD, 1).astype(BF)
        sent[1, rows, :] = pltpu.roll(dvs[other, :], HD, 1).astype(BF)


def attend_back(tiles, blocks, table, q, k_own, v_own, k_other, v_other, cot, att, log_in):
    tokens = q.shape[0]
    keys = blocks * BLK
    return pl.pallas_call(
        functools.partial(attend_back_kernel, tiles, blocks),
        out_shape=(
            jax.ShapeDtypeStruct((tokens, 128), F32),
            jax.ShapeDtypeStruct((keys // 2, 128), F32),
            jax.ShapeDtypeStruct((keys // 2, 128), F32),
            jax.ShapeDtypeStruct((2, keys // 2, 128), BF),
        ),
        in_specs=[pl.BlockSpec(memory_space=pltpu.SMEM)] + full_spec(8),
        out_specs=tuple(full_spec(4)),
        scratch_shapes=[
            pltpu.VMEM((tokens, 128), BF),
            pltpu.VMEM((keys, 128), BF),
            pltpu.VMEM((keys, 128), BF),
            pltpu.VMEM((tokens, 128), BF),
            pltpu.VMEM((tokens, 128), F32),
            pltpu.VMEM((tokens, 128), F32),
            pltpu.VMEM((tokens, 128), F32),
            pltpu.VMEM((keys, 128), F32),
            pltpu.VMEM((keys, 128), F32),
        ],
        cost_estimate=pl.CostEstimate(
            flops=20 * 256 * 128 * sum(tiles),
            bytes_accessed=6000000,
            transcendentals=256 * sum(tiles),
        ),
        name="attend_back",
    )(table, q, k_own, v_own, k_other, v_other, cot, att, log_in)


def front_kernel(
    place,
    firsts,
    firsts_y,
    seconds,
    seconds_x,
    gain,
    shift,
    qkv,
    bias_joint,
    cosine,
    sine_a,
    sine_b,
    fc1_own,
    fc1_other,
    bias1,
    normed,
    mean,
    inv,
    queries,
    keys,
    values,
    sent,
    pre,
    active,
):
    sides = sides_of(place)
    rows = [
        part.astype(F32)
        for part in piece_rows(pl.program_id(0), firsts, firsts_y, seconds, seconds_x)
    ]
    center = sum(jnp.sum(part, axis=-1, keepdims=True) for part in rows) / D
    rows = [part - center for part in rows]
    spread_ = sum(jnp.sum(part * part, axis=-1, keepdims=True) for part in rows) / D
    inv_std = lax.rsqrt(spread_ + epsilon)
    mean[...] = jnp.broadcast_to(center, mean.shape)
    inv[...] = jnp.broadcast_to(inv_std, inv.shape)
    for part, side in zip(rows, sides):
        normed[:, side] = (part * inv_std * gain[:, side] + shift[:, side]).astype(BF)
    normed16 = normed[...]
    joint = dot(normed16, qkv[...], 1, 0) + bias_joint[...]
    tables = (cosine[...], sine_a[...], sine_b[...])
    queries[...] = turn(joint[:, :BLK], *tables).astype(BF)
    turned, value = turn(joint[:, BLK : 2 * BLK], *tables), joint[:, 2 * BLK :]
    keys[...] = turned.astype(BF)
    values[...] = value.astype(BF)
    sent[0] = pltpu.roll(turned, HD, 1).astype(BF)
    sent[1] = pltpu.roll(value, HD, 1).astype(BF)
    hidden = fc1_own.shape[1]
    for part, weight in enumerate((fc1_own, fc1_other)):
        columns = slice(part * hidden, (part + 1) * hidden)
        result = dot(normed16, weight[...], 1, 0) + bias1[:, columns]
        pre[:, columns] = result
        inner = jnp.tanh(inner_coef * (result + cubic_coef * result * result * result))
        active[:, columns] = (0.5 * result * (1.0 + inner)).astype(BF)


def front(place, pieces, gain, shift, qkv, bias_joint, cosine, sine_a, sine_b, fc1_own, fc1_other, bias1):
    tokens = LO * BLK
    hidden = fc1_own.shape[1]

    def shape(columns, dtype):
        return jax.ShapeDtypeStruct((tokens, columns), dtype)

    narrow = rows_spec(BLK)
    return pl.pallas_call(
        front_kernel,
        grid=(tokens // STEP,),
        out_shape=(
            shape(D, BF),
            shape(BLK, F32),
            shape(BLK, F32),
            shape(BLK, BF),
            shape(BLK, BF),
            shape(BLK, BF),
            jax.ShapeDtypeStruct((2, tokens, BLK), BF),
            shape(2 * hidden, F32),
            shape(2 * hidden, BF),
        ),
        in_specs=[
            scalar_spec(),
            *piece_specs(),
            fixed_spec(1, D),
            fixed_spec(1, D),
            fixed_spec(D, 3 * BLK),
            fixed_spec(1, 3 * BLK),
            narrow,
            narrow,
            narrow,
            fixed_spec(D, hidden),
            fixed_spec(D, hidden),
            fixed_spec(1, 2 * hidden),
        ],
        out_specs=(
            rows_spec(D),
            narrow,
            narrow,
            narrow,
            narrow,
            narrow,
            pl.BlockSpec((2, STEP, BLK), lambda i: (0, i, 0)),
            rows_spec(2 * hidden),
            rows_spec(2 * hidden),
        ),
        cost_estimate=cost(2 * tokens * D * (384 + 2 * hidden), 12 * tokens * D // 2),
        name="front",
    )(
        place,
        *pieces,
        gain,
        shift,
        qkv,
        bias_joint,
        cosine,
        sine_a,
        sine_b,
        fc1_own,
        fc1_other,
        bias1,
    )


def store_pieces(step, index, rows, a_own, a_other, b_near, b_far):
    for s in range(2):
        (a_own, a_other)[index][s] = rows[s * BLK : s * BLK + HALF]
    for wanted, target in ((step < 2, b_near), (step >= 2, b_far)):

        @pl.when(wanted)
        def _(target=target):
            for s in range(2):
                target[s, index] = rows[s * BLK + HALF : (s + 1) * BLK]


def partial_shapes():
    return (
        jax.ShapeDtypeStruct((LO, HALF, UNIT), BF),
        jax.ShapeDtypeStruct((LO, HALF, UNIT), BF),
        jax.ShapeDtypeStruct((LO // 2, 2, HALF, UNIT), BF),
        jax.ShapeDtypeStruct((LO // 2, 2, HALF, UNIT), BF),
    )


def partial_specs():
    near = pl.BlockSpec((2, HALF, UNIT), lambda i: (i, 0, 0))
    return (
        near,
        near,
        pl.BlockSpec((2, 2, HALF, UNIT), lambda i: (jnp.minimum(i, 1), 0, 0, 0)),
        pl.BlockSpec((2, 2, HALF, UNIT), lambda i: (jnp.maximum(i - 2, 0), 0, 0, 0)),
    )


def mix_kernel(place, attended, active, out2, fc2_own, fc2_other, *partial):
    hidden = fc2_own.shape[1]
    for index, side in enumerate((place[0], 1 - place[0])):
        parts = []
        for quarter in range(4):
            c = 4 * side + quarter
            parts.append(
                (
                    dot(active[:, :hidden], fc2_own[c], 1, 0)
                    + dot(active[:, hidden:], fc2_other[c], 1, 0)
                    + dot(attended[...], out2[c], 1, 0)
                ).astype(BF)
            )
        store_pieces(pl.program_id(0), index, jnp.concatenate(parts, axis=1), *partial)


def mix(place, attended, active, out2, fc2_own, fc2_other):
    tokens = LO * BLK
    hidden = fc2_own.shape[1]
    return pl.pallas_call(
        mix_kernel,
        grid=(tokens // STEP,),
        out_shape=partial_shapes(),
        in_specs=[
            scalar_spec(),
            rows_spec(BLK),
            rows_spec(2 * hidden),
            fixed_spec(LO, BLK, 256),
            fixed_spec(LO, hidden, 256),
            fixed_spec(LO, hidden, 256),
        ],
        out_specs=partial_specs(),
        cost_estimate=cost(2 * tokens * D * (128 + 2 * hidden), 8000000),
        name="mix",
    )(place, attended, active, out2, fc2_own, fc2_other)


def back_kernel(
    place,
    firsts,
    firsts_y,
    seconds,
    seconds_x,
    pre,
    out2,
    fc2_own,
    fc2_other,
    cot,
    grad_pre,
    grad_attended,
    bias_sum,
):
    @pl.when(pl.program_id(0) == 0)
    def _():
        bias_sum[...] = jnp.zeros_like(bias_sum)

    parts = piece_rows(pl.program_id(0), firsts, firsts_y, seconds, seconds_x)
    for part, side in zip(parts, sides_of(place)):
        cot[:, side] = part
    rows = cot[...]
    hidden = fc2_own.shape[1]

    def through(weight):
        total = 0.0
        for c in range(LO):
            total = total + dot(rows[:, c * 256 : (c + 1) * 256], weight[c], 1, 1)
        return total

    grad_attended[...] = through(out2).astype(BF)
    for part, weight in enumerate((fc2_own, fc2_other)):
        columns = slice(part * hidden, (part + 1) * hidden)
        value = pre[:, columns]
        inner = jnp.tanh(inner_coef * (value + cubic_coef * value * value * value))
        slope = 0.5 * (1.0 + inner) + 0.5 * value * (1.0 - inner * inner) * inner_coef * (
            1.0 + 3.0 * cubic_coef * value * value
        )
        grad = through(weight) * slope
        bias_sum[:, columns] += jnp.sum(grad, axis=0, keepdims=True)
        grad_pre[:, columns] = grad.astype(BF)


def back(place, pieces, pre, out2, fc2_own, fc2_other):
    tokens = LO * BLK
    hidden = fc2_own.shape[1]
    return pl.pallas_call(
        back_kernel,
        grid=(tokens // STEP,),
        out_shape=(
            jax.ShapeDtypeStruct((tokens, D), BF),
            jax.ShapeDtypeStruct((tokens, 2 * hidden), BF),
            jax.ShapeDtypeStruct((tokens, BLK), BF),
            jax.ShapeDtypeStruct((1, 2 * hidden), F32),
        ),
        in_specs=[
            scalar_spec(),
            *piece_specs(),
            rows_spec(2 * hidden),
            fixed_spec(LO, BLK, 256),
            fixed_spec(LO, hidden, 256),
            fixed_spec(LO, hidden, 256),
        ],
        out_specs=(
            rows_spec(D),
            rows_spec(2 * hidden),
            rows_spec(BLK),
            fixed_spec(1, 2 * hidden),
        ),
        cost_estimate=cost(2 * tokens * D * (128 + 2 * hidden), 14000000),
        name="back",
    )(place, *pieces, pre, out2, fc2_own, fc2_other)


def unturn_kernel(dq, dk, dv, got, cosine, sine_a, sine_b, joint, own, other, bias):
    tables = (cosine[...], -sine_a[...], -sine_b[...])
    dk_all = dk[...] + got[0].astype(F32)
    dv_all = dv[...] + got[1].astype(F32)
    for j, grads in enumerate((turn(dq[...], *tables), turn(dk_all, *tables), dv_all)):
        columns = slice(j * BLK, (j + 1) * BLK)
        bias[:, columns] = jnp.sum(grads, axis=0, keepdims=True)
        grads = grads.astype(BF)
        joint[:, columns] = grads
        own[:, j * HD : (j + 1) * HD] = grads[:, :HD]
        other[:, j * HD : (j + 1) * HD] = grads[:, HD:]


def unturn(dq, dk, dv, got, cosine, sine_a, sine_b):
    tokens = dq.shape[0]
    return pl.pallas_call(
        unturn_kernel,
        out_shape=(
            jax.ShapeDtypeStruct((tokens, 3 * BLK), BF),
            jax.ShapeDtypeStruct((tokens, 3 * HD), BF),
            jax.ShapeDtypeStruct((tokens, 3 * HD), BF),
            jax.ShapeDtypeStruct((1, 3 * BLK), F32),
        ),
        in_specs=full_spec(7),
        out_specs=tuple(full_spec(4)),
        cost_estimate=cost(0, 6000000),
        name="unturn",
    )(dq, dk, dv, got, cosine, sine_a, sine_b)


def grad_kernel(
    place,
    firsts,
    firsts_y,
    seconds,
    seconds_x,
    mean,
    inv,
    gain,
    joint,
    grad_pre,
    qkv,
    fc1_own,
    fc1_other,
    a_own,
    a_other,
    b_near,
    b_far,
    sums,
    gain_sum,
    shift_sum,
):
    step = pl.program_id(0)

    @pl.when(step == 0)
    def _():
        gain_sum[...] = jnp.zeros_like(gain_sum)
        shift_sum[...] = jnp.zeros_like(shift_sum)

    hidden = fc1_own.shape[1]
    parts = piece_rows(step, firsts, firsts_y, seconds, seconds_x)
    first, second = 0.0, 0.0
    for index, (side, part) in enumerate(zip(sides_of(place), parts)):
        grads = (
            dot(joint[...], qkv[side, :], 1, 1)
            + dot(grad_pre[:, :hidden], fc1_own[side, :], 1, 1)
            + dot(grad_pre[:, hidden:], fc1_other[side, :], 1, 1)
        )
        store_pieces(step, index, grads.astype(BF), a_own, a_other, b_near, b_far)
        both = grads * ((part.astype(F32) - mean[:, :1]) * inv[:, :1])
        shift_sum[index : index + 1, :] += jnp.sum(grads, axis=0, keepdims=True)
        gain_sum[index : index + 1, :] += jnp.sum(both, axis=0, keepdims=True)
        first = first + jnp.sum(grads * gain[:, side], axis=-1, keepdims=True)
        second = second + jnp.sum(both * gain[:, side], axis=-1, keepdims=True)
    lane = lax.broadcasted_iota(jnp.int32, (STEP, BLK), 1)
    turned = jnp.transpose(jnp.where(lane < HD, first, second))
    sums[0:1, :] = turned[0:1]
    sums[1:2, :] = turned[HD : HD + 1]


def grad_units(place, pieces, mean, inv, gain, joint, grad_pre, qkv, fc1_own, fc1_other):
    tokens = LO * BLK
    hidden = fc1_own.shape[1]
    return pl.pallas_call(
        grad_kernel,
        grid=(tokens // STEP,),
        out_shape=(
            *partial_shapes(),
            jax.ShapeDtypeStruct((2, tokens), F32),
            jax.ShapeDtypeStruct((2, UNIT), F32),
            jax.ShapeDtypeStruct((2, UNIT), F32),
        ),
        in_specs=[
            scalar_spec(),
            *piece_specs(),
            rows_spec(BLK),
            rows_spec(BLK),
            fixed_spec(1, D),
            rows_spec(3 * BLK),
            rows_spec(2 * hidden),
            fixed_spec(D, 3 * BLK),
            fixed_spec(D, hidden),
            fixed_spec(D, hidden),
        ],
        out_specs=(
            *partial_specs(),
            pl.BlockSpec((2, STEP), lambda i: (0, i)),
            fixed_spec(2, UNIT),
            fixed_spec(2, UNIT),
        ),
        cost_estimate=cost(2 * tokens * D * (384 + 2 * hidden), 16000000),
        name="grad",
    )(place, *pieces, mean, inv, gain, joint, grad_pre, qkv, fc1_own, fc1_other)


def step_body(
    n_hi,
    layer_input,
    norm_gain,
    norm_shift,
    w_qkv,
    b_qkv,
    w_out,
    b_out,
    w_fc1,
    b_fc1,
    w_fc2,
    b_fc2,
    grad_output,
    placement,
    position_ids,
):
    hi, y, k = (lax.axis_index(name) for name in ("hi", "y", "k"))
    lo = lax.axis_index(LOX)
    depth = D // (n_hi * LO)
    width = w_qkv.shape[2]
    hidden = w_fc1.shape[1] // LO
    tokens = LO * BLK

    def half(values, which):
        split = values.reshape((2, 2, HALF) + values.shape[1:])
        cut = lax.dynamic_index_in_dim(split, which, 1, keepdims=False)
        return cut.reshape((BLK,) + values.shape[1:])

    def in_order(index, own, got, axis):
        return jnp.where(
            index == 0,
            jnp.concatenate([own, got], axis=axis),
            jnp.concatenate([got, own], axis=axis),
        )

    def make_unit(values):
        got = swap(half(values, 1 - k), "k")
        return in_order(k, half(values, k), got, 1)

    unit_in = make_unit(layer_input)
    pieces = gather_pieces(unit_in)
    unit_cot = make_unit(grad_output)
    pieces_cot = gather_pieces(unit_cot)
    ids = half(position_ids, k)
    for name in ("zh", "zl", "x"):
        ids = jnp.stack([ids, swap(ids, name)])
    ids, w_fc1, w_qkv, w_fc2, w_out = lax.optimization_barrier((ids, w_fc1, w_qkv, w_fc2, w_out))
    slot_lo = [lo ^ (((s & 1) << 2) | (s & 2) | (s >> 2)) for s in range(LO)]
    place = jnp.stack([y, k] + slot_lo).astype(jnp.int32)

    def over_hi(values):
        return values[None] if n_hi == 1 else lax.all_gather(values, "hi", axis=0)

    def ordered(got, shape):
        return got if n_hi == 1 else jnp.moveaxis(got, 1, 0).reshape(shape)

    fc1_own = spread(over_hi(w_fc1).reshape(n_hi, depth, LO, hidden).transpose(2, 0, 1, 3))
    fc1_own = ordered(fc1_own, (D, hidden)).reshape(D, hidden)
    fc1_other = swap(fc1_own, "k")
    down = jnp.concatenate(
        [w_fc2.reshape(LO, hidden, depth), w_out.reshape(LO, HD, depth)], axis=1
    )
    down = spread(jnp.moveaxis(over_hi(down), 0, 1))
    if n_hi == 1:
        down_own = down.reshape(LO, hidden + HD, 256)
    else:
        down_own = down.transpose(2, 1, 0, 3).reshape(hidden + HD, LO, 256).transpose(1, 0, 2)
    down_other = swap(down_own, "k")
    fc2_own, fc2_other = down_own[:, :hidden], down_other[:, :hidden]
    out2 = jnp.concatenate([down_own[:, hidden:], down_other[:, hidden:]], axis=1)
    if n_hi == 1:
        heads_own = spread(pack_heads(w_qkv.transpose(1, 0, 2)))
        qkv = join_heads(heads_own, swap(heads_own, "k"))
    else:
        cut = over_hi(w_qkv).reshape(n_hi, depth, 3, LO, HD).transpose(3, 0, 1, 2, 4)
        heads_own = spread(cut.reshape(LO, n_hi, depth, 3 * HD))
        heads_own = ordered(heads_own, (D, 3, HD))
        qkv = jnp.concatenate([heads_own, swap(heads_own, "k")], axis=2).reshape(D, 6 * HD)

    own_head = lax.dynamic_slice_in_dim(b_qkv, lo * HD, HD, 1)
    own_bias1 = lax.dynamic_slice_in_dim(b_fc1, lo * hidden, hidden, 0)
    affine = jnp.stack([norm_gain.astype(F32), norm_shift.astype(F32)])
    small = jnp.concatenate([affine.reshape(-1), own_head.reshape(-1), own_bias1])
    small_other = swap(small, "k")
    affine = in_order(k, affine, small_other[: 2 * width].reshape(2, width), 1)
    affine = in_order(y, affine, swap(affine, "y"), 1)
    gain, shift = affine[0:1], affine[1:2]
    head_other = small_other[2 * width : 2 * width + 3 * HD].reshape(3, HD)
    bias_joint = jnp.concatenate([own_head, head_other], axis=1).reshape(1, 6 * HD)
    bias1 = jnp.concatenate([own_bias1, small_other[2 * width + 3 * HD :]])[None]

    ids = ids.reshape(tokens)
    lane = jnp.arange(BLK, dtype=jnp.int32) % HD
    frequency = 10000.0 ** (-2.0 * (lane % (ROT // 2)).astype(F32) / ROT)
    angles = ids.astype(F32)[:, None] * frequency[None, :]
    cosine = jnp.where(lane < ROT, jnp.cos(angles), 1.0)
    sine = jnp.sin(angles)
    sine_a = jnp.where(lane < ROT // 2, -sine, 0.0)
    sine_b = jnp.where((lane >= ROT // 2) & (lane < ROT), sine, 0.0)

    blocks = n_hi * 2 * LO
    by_group = placement.reshape(n_hi, LO, 2)
    in_slots = jnp.stack(
        [lax.dynamic_index_in_dim(by_group, c, 1, keepdims=False) for c in slot_lo], axis=1
    ).reshape(n_hi, 2 * LO)
    local = lax.dynamic_index_in_dim(in_slots, hi, 0, keepdims=False)
    ranks = jnp.sum((local[None, :] < local[:, None]).astype(jnp.int32), axis=1)
    sorted_local = jnp.sort(local) if n_hi > 1 else jnp.arange(2 * LO, dtype=jnp.int32)
    table = jnp.concatenate(
        [k[None].astype(jnp.int32), in_slots.reshape(-1), ranks, sorted_local]
    )
    if n_hi == 1:
        tiles = tuple(4 * BLK * (m // 2 + 1) for m in range(LO))
    else:
        tiles = (blocks * BLK,) * LO

    normed16, mean, inv, queries, keys, values, sent, pre, active = front(
        place,
        pieces,
        gain,
        shift,
        qkv,
        bias_joint,
        cosine,
        sine_a,
        sine_b,
        fc1_own,
        fc1_other,
        bias1,
    )
    other_kv = swap(sent, "k")

    def all_keys(rows):
        return rows if n_hi == 1 else lax.all_gather(rows, "hi", axis=0, tiled=True)

    key_set = tuple(all_keys(v) for v in (keys, values, other_kv[0], other_kv[1]))
    attended, log_total = attend(tiles, blocks, table, queries, *key_set)
    summed = scatter_pieces(*mix(place, attended, active, out2, fc2_own, fc2_other))

    cot, grad_pre, grad_attended, term_bias1 = back(place, pieces_cot, pre, out2, fc2_own, fc2_other)

    def summed_dot(left, own, other, flip):
        def product(right):
            return dot(right, left, 0, 0) if flip else dot(left, right, 0, 0)

        return product(own), swap(product(other).astype(BF), "k")

    def home(total):
        got = spread(total)
        if n_hi == 1:
            return got[:, 0]
        return lax.psum_scatter(got.astype(F32), "hi", scatter_dimension=1)

    def add(own, got):
        return (own + got.astype(F32)).astype(BF)

    def cut_columns(values):
        rows = values.shape[0]
        return values.reshape(rows, n_hi, LO, depth).transpose(2, 1, 0, 3)

    fc2_sum = add(*summed_dot(cot, active[:, :hidden], active[:, hidden:], True))
    out_sum = add(*summed_dot(cot, attended[:, :HD], attended[:, HD:], True))
    down = jnp.concatenate([cut_columns(fc2_sum), cut_columns(out_sum)], axis=2)
    fc1_term, fc1_got = summed_dot(normed16, grad_pre[:, :hidden], grad_pre[:, hidden:], False)
    if n_hi == 1:
        grad_attended, down, fc1_term, fc1_got = lax.optimization_barrier(
            (grad_attended, down, fc1_term, fc1_got)
        )
    down_home = home(down)
    grad_fc2 = down_home[:, :hidden].reshape(LO * hidden, depth).astype(F32)
    grad_out = down_home[:, hidden:].reshape(LO * HD, depth).astype(F32)

    dq, dk, dv, grads_sent = attend_back(
        tiles, blocks, table, queries, *key_set, grad_attended, attended, log_total
    )

    def own_keys(rows):
        if n_hi == 1:
            return rows
        return lax.psum_scatter(rows, "hi", scatter_dimension=0, tiled=True)

    got = swap(grads_sent, "k")
    if n_hi > 1:
        dk = own_keys(dk + got[0].astype(F32))
        dv = own_keys(dv + got[1].astype(F32))
        got = jnp.zeros((2,) + dk.shape, BF)
    joint, joint_own, joint_other, term_joint_bias = unturn(
        dq, dk, dv, got, cosine, sine_a, sine_b
    )
    own_term, got_term = summed_dot(normed16, joint_own, joint_other, False)
    if n_hi == 1:
        packed = pack_grads(fc1_term, fc1_got, own_term, got_term)
        packed, joint = lax.optimization_barrier((packed, joint))
        grad_fc1, grad_qkv = home_grads(spread(packed))
        grad_qkv = grad_qkv.transpose(1, 0, 2)
    else:
        fc1_sum = add(fc1_term, fc1_got).reshape(n_hi, LO, depth, hidden)
        fc1_home = home(fc1_sum.transpose(1, 0, 2, 3))
        grad_fc1 = fc1_home.transpose(1, 0, 2).reshape(depth, LO * hidden).astype(F32)
        qkv_sum = add(own_term, got_term).reshape(n_hi, LO, depth, 3 * HD)
        qkv_home = home(qkv_sum.transpose(1, 0, 2, 3)).reshape(LO, depth, 3, HD)
        grad_qkv = qkv_home.transpose(1, 2, 0, 3).reshape(depth, 3, width).astype(F32)
    *partial, row_sums, gain_sum, shift_sum = grad_units(
        place, pieces, mean, inv, gain, joint, grad_pre, qkv, fc1_own, fc1_other
    )
    grad_unit = scatter_pieces(*partial)

    heads = lax.dynamic_update_slice(
        jnp.zeros((2, 3, width), F32),
        term_joint_bias.reshape(3, 2, HD).transpose(1, 0, 2),
        (0, 0, lo * HD),
    )
    bias_sum = lax.dynamic_update_slice(
        jnp.zeros((2, LO * hidden), F32), term_bias1.reshape(2, hidden), (0, lo * hidden)
    )
    affine_sum = jnp.stack([gain_sum, shift_sum]).reshape(2, 2, 2, width).transpose(1, 2, 0, 3)

    def pick(values, index):
        return lax.dynamic_index_in_dim(values, index, 0, keepdims=False)

    row_pair = row_sums.reshape(-1)
    over_y = jnp.concatenate([affine_sum[1].reshape(-1), row_pair])
    over_y = swap(over_y, "y")
    affine_sum = affine_sum[0] + over_y[: 4 * width].reshape(2, 2, width)
    row_pair = (row_pair + over_y[4 * width :]).reshape(2, tokens)
    over_k = jnp.concatenate(
        [heads[1].reshape(-1), bias_sum[1], pick(affine_sum, 1 - k).reshape(-1)]
    )
    over_k = swap(over_k, "k") + jnp.concatenate(
        [heads[0].reshape(-1), bias_sum[0], pick(affine_sum, k).reshape(-1)]
    )
    local_bias = jnp.sum(grad_output.astype(F32), axis=0)
    flat = jnp.concatenate([over_k, local_bias])
    length = flat.shape[0]
    for name in ("x", "zl", "zh"):
        left = row_pair.shape[1] // 2
        got = swap(jnp.concatenate([flat, row_pair[:, left:].reshape(-1)]), name)
        flat = flat + got[:length]
        row_pair = row_pair[:, :left] + got[length:].reshape(2, left)
    row_own = row_pair.T / D
    if n_hi > 1:
        flat = lax.psum(flat, "hi")
    cuts = [3 * width, LO * hidden, width, width, width]
    ends = [sum(cuts[: i + 1]) for i in range(len(cuts))]
    grad_b_qkv = flat[: ends[0]].reshape(3, width)
    grad_b_fc1 = flat[ends[0] : ends[1]]
    grad_gain = flat[ends[1] : ends[2]]
    grad_shift = flat[ends[2] : ends[3]]
    grad_b_out = flat[ends[3] :]

    def to_rows(unit):
        parts = unit.reshape(BLK, 2, width)
        own = lax.dynamic_index_in_dim(parts, k, 1, keepdims=False)
        got = swap(lax.dynamic_index_in_dim(parts, 1 - k, 1, keepdims=False), "k")
        own, got = own.reshape(2, 1, HALF, width), got.reshape(2, 1, HALF, width)
        return in_order(k, own, got, 1).reshape(2 * BLK, width)

    layer_output = layer_input.astype(F32) + to_rows(summed) + b_out + b_fc2

    mean_own, inv_own = mean[:BLK, :1], inv[:BLK, :1]
    gain_own = lax.dynamic_slice_in_dim(gain, y * UNIT, UNIT, 1)
    normed_unit = (unit_in.astype(F32) - mean_own) * inv_own
    grad_x = inv_own * (
        grad_unit * gain_own - row_own[:, :1] - normed_unit * row_own[:, 1:]
    )
    grad_input = to_rows(grad_x + unit_cot.astype(F32))
    return (
        layer_output,
        grad_input,
        grad_gain,
        grad_shift,
        grad_qkv,
        grad_b_qkv,
        grad_out,
        grad_b_out,
        grad_fc1,
        grad_b_fc1,
        grad_fc2,
        grad_b_out,
    )


def on_device(n_hi, *arguments):
    return step_body(n_hi, *arguments)


def solution(mesh):
    n_hi = mesh.shape["ctx"] // LO
    inner = Mesh(mesh.devices.reshape(n_hi, 2, 2, 2, 2, 2), CTX + TP)
    in_specs = (
        P(CTX, TP),
        P(TP),
        P(TP),
        P(CTX, None, TP),
        P(None, TP),
        P(TP, CTX),
        P(TP),
        P(CTX, TP),
        P(TP),
        P(TP, CTX),
        P(TP),
        P(CTX, TP),
        P(),
        P(CTX),
    )
    out_specs = (
        P(CTX, TP),
        P(CTX, TP),
        P(TP),
        P(TP),
        P(CTX, None, TP),
        P(None, TP),
        P(TP, CTX),
        P(TP),
        P(CTX, TP),
        P(TP),
        P(TP, CTX),
        P(TP),
    )
    return jax.shard_map(
        functools.partial(on_device, n_hi),
        mesh=inner,
        in_specs=in_specs,
        out_specs=out_specs,
        check_vma=False,
    )
```

profile of v0, /device:TPU:0, one launch (start us, length us, event | category | flops | bytes accessed | tf_op | source)
XLA Modules:
  0.0 451.1 jit_solution(8785813738179335506)
XLA Ops:
  2.8 4.1 collective-permute-start.9
  18.5 6.1 %all-to-all-start = ((bf16[8,3,128,128]{3,2,1,0:T(8,128)(2,1)}), bf16[8,3,128,128]{3,2,1,0:T(8,128)(2,1)S(1)}, u32[]{:S(2)}, u32[]{:S(2)}) async-start(bf16[8,3,128,128]{3,2,1,0:T(8,128)(2,1)} %pack.1), calls=%async_computation | async-start | bytes 1572864 | tf_op jit(solution)/shard_map/all_to_all | solution.py:37
  27.2 14.4 %all-to-all-done.own = bf16[8,3,128,128]{3,2,1,0:T(8,128)(2,1)S(1)} async-done(((bf16[8,3,128,128]{3,2,1,0:T(8,128)(2,1)}), bf16[8,3,128,128]{3,2,1,0:T(8,128)(2,1)S(1)}, u32[]{:S(2)}, u32[]{:S(2)}) %all-to-all-start) | async-done | bytes 786464 | tf_op jit(solution)/shard_map/all_to_all | solution.py:37
  41.5 4.2 all-to-all-start.1
  53.4 27.7 %collective-permute-done.1 = bf16[2,64,1024]{2,1,0:T(8,128)(2,1)S(1)} collective-permute-done((bf16[2,64,1024]{2,1,0:T(8,128)(2,1)S(1)}, bf16[2,64,1024]{2,1,0:T(8,128)(2,1)S(1)}, u32[]{:S(2)}, u32[]{:S(2)}) %collective-permute-start.1) | collective-permute-done | bytes 262176 | tf_op jit(solution)/shard_map/ppermute | solution.py:33
  87.1 10.1 %collective-permute-done.24 = bf16[2,64,1024]{2,1,0:T(8,128)(2,1)S(1)} collective-permute-done((bf16[2,64,1024]{2,1,0:T(8,128)(2,1)S(1)}, bf16[2,64,1024]{2,1,0:T(8,128)(2,1)S(1)}, u32[]{:S(2)}, u32[]{:S(2)}) %collective-permute-start.24) | collective-permute-done | bytes 262176 | tf_op jit(solution)/shard_map/ppermute | solution.py:33
  102.4 4.8 %all-to-all-start.2 = ((bf16[8,1,320,256]{3,2,1,0:T(8,128)(2,1)}), bf16[8,1,320,256]{3,2,1,0:T(8,128)(2,1)S(1)}, u32[]{:S(2)}, u32[]{:S(2)}) async-start(bf16[8,1,320,256]{3,2,1,0:T(8,128)(2,1)} %maximum_bitcast_fusion), calls=%async_computation.2 | async-start | bytes 2621440 | tf_op jit(solution)/shard_map/all_to_all | solution.py:37
  110.2 3.2 fusion.4
  119.3 5.4 %collective-permute-start.26 = (bf16[4,64,1024]{2,1,0:T(8,128)(2,1)}, bf16[4,64,1024]{2,1,0:T(8,128)(2,1)}, u32[]{:S(2)}, u32[]{:S(2)}) collective-permute-start(bf16[4,64,1024]{2,1,0:T(8,128)(2,1)} %get-tuple-element.111), channel_id=1, source_target_pairs={{0,4},{4,0},{1,5},{5,1},{2,6},{6,2},{3,7},{7,3},{8,12},{12,8},{9,1... | collective-permute-start | bytes 1572872 | tf_op jit(solution)/shard_map/ppermute | solution.py:33
  126.8 9.9 %collective-permute-done.3 = bf16[4,64,1024]{2,1,0:T(8,128)(2,1)S(1)} collective-permute-done((bf16[4,64,1024]{2,1,0:T(8,128)(2,1)}, bf16[4,64,1024]{2,1,0:T(8,128)(2,1)S(1)}, u32[]{:S(2)}, u32[]{:S(2)}) %collective-permute-start.3) | collective-permute-done | bytes 524320 | tf_op jit(solution)/shard_map/ppermute | solution.py:33
  142.7 15.3 %collective-permute-done.8 = f32[2,1024]{1,0:T(2,128)S(1)} collective-permute-done((f32[2,1024]{1,0:T(2,128)S(1)}, f32[2,1024]{1,0:T(2,128)S(1)}, u32[]{:S(2)}, u32[]{:S(2)}) %collective-permute-start.8) | collective-permute-done | bytes 8224 | tf_op jit(solution)/shard_map/ppermute | solution.py:33
  168.8 13.1 %front.1 = (bf16[1024,2048]{1,0:T(8,128)(2,1)}, f32[1024,128]{1,0:T(8,128)}, f32[1024,128]{1,0:T(8,128)}, bf16[1024,128]{1,0:T(8,128)(2,1)}, bf16[1024,128]{1,0:...) custom-call(s32[10]{0:T(128)} %stack.155.place, ...), custom_call_target="tpu_custom_call" | custom-call | flops 3758096384 | bytes 12582912 | tf_op jit(solution)/shard_map/front/pallas_call | solution.py:541
  193.2 9.8 %attend.1 = (bf16[1024,128]{1,0:T(8,128)(2,1)}, f32[1024,128]{1,0:T(8,128)}) custom-call(s32[49]{0:T(128)} %pad_add_fusion.3.table, bf16[1024,128]{1,0:T(8,128)(2,1)} %get-tuple-element.62.q, bf16[1024,128]{1,0:T(8,128)(2,1)} %get-tuple-element.63.k_own, bf16[1024,128]{1,0:T(8,128)(2,1)} %get-tuple-element.64.v_own, ...), custom_call_target="tpu_custom_call" | custom-call | flops 2684354560 | bytes 2000000 | tf_op jit(solution)/shard_map/attend/pallas_call | solution.py:314
  205.0 5.0 %collective-permute-done.29.seconds_x = bf16[2,4,64,1024]{3,2,1,0:T(8,128)(2,1)} collective-permute-done((bf16[2,4,64,1024]{3,2,1,0:T(8,128)(2,1)}, bf16[2,4,64,1024]{3,2,1,0:T(8,128)(2,1)}, u32[]{:S(2)}, u32[]{:S(2)}) %collective-permute-start.29) | collective-permute-done | bytes 1048608 | tf_op jit(solution)/shard_map/ppermute | solution.py:33
  210.0 9.3 %back.1 = (bf16[1024,2048]{1,0:T(8,128)(2,1)}, bf16[1024,512]{1,0:T(8,128)(2,1)}, bf16[1024,128]{1,0:T(8,128)(2,1)}, f32[1,512]{1,0:T(1,128)}) custom-call(s32[10]{0:T(128)} %stack.155.place, bf16[2,4,64,1024]{3,2,1,0:T(8,128)(2,1)} %pad_maximum_fusion.5.firsts, bf16[2,4,64,1024]{3,2,1,0:T(8,128)(2,1)} %collective-permute-done.27.firsts_y, ...), custom_call_target="tpu_custom_call" | custom-call | flops 2684354560 | bytes 14000000 | tf_op jit(solution)/shard_map/back/pallas_call | solution.py:712
  219.3 4.8 %convolution_convert_fusion = bf16[2048,256]{1,0:T(8,128)(2,1)} fusion(bf16[1024,2048]{1,0:T(8,128)(2,1)} %get-tuple-element.79, bf16[1024,512]{1,0:T(8,128)(2,1)} %get-tuple-element.80.grad_pre), kind=kOutput, calls=%fused_computation.2 | convolution fusion | flops 1074266112 | bytes 5767168 | tf_op jit(solution)/shard_map/dot_general | solution.py:69
  232.6 8.1 %mix.1 = (bf16[8,64,1024]{2,1,0:T(8,128)(2,1)}, bf16[8,64,1024]{2,1,0:T(8,128)(2,1)}, bf16[4,2,64,1024]{3,2,1,0:T(8,128)(2,1)}, bf16[4,2,64,1024]{3,2,1,0:T(8,128)(2,1)}) custom-call(s32[10]{0:T(128)} %stack.155.place, bf16[1024,128]{1,0:T(8,128)(2,1)} %get-tuple-element.66.attended.att, bf16[1024,512]{1,0:T(8,128)(2,1)} %get-tuple-element.67.active, ...), custom_call_target="tpu_custom_call" | custom-call | flops 2684354560 | bytes 8000000 | tf_op jit(solution)/shard_map/mix/pallas_call | solution.py:647
  242.9 3.5 fusion.1
  250.8 12.4 %attend_back.1 = (f32[1024,128]{1,0:T(8,128)}, f32[1024,128]{1,0:T(8,128)}, f32[1024,128]{1,0:T(8,128)}, bf16[2,1024,128]{2,1,0:T(8,128)(2,1)}) custom-call(s32[49]{0:T(128)} %pad_add_fusion.3.table, bf16[1024,128]{1,0:T(8,128)(2,1)} %get-tuple-element.62.q, bf16[1024,128]{1,0:T(8,128)(2,1)} %get-tuple-element.63.k_own, ...), custom_call_target="tpu_custom_call" | custom-call | flops 6710886400 | bytes 6000000 | tf_op jit(solution)/shard_map/attend_back/pallas_call | solution.py:446
  263.2 5.0 %all-to-all-start.4 = ((bf16[8,1,320,256]{3,2,1,0:T(8,128)(2,1)}), bf16[8,1,320,256]{3,2,1,0:T(8,128)(2,1)S(1)}, u32[]{:S(2)}, u32[]{:S(2)}) async-start(bf16[8,1,320,256]{3,2,1,0:T(8,128)(2,1)} %pad_maximum_fusion), calls=%async_computation.4 | async-start | bytes 2621440 | tf_op jit(solution)/shard_map/all_to_all | solution.py:37
  277.2 4.3 unturn.1
  281.5 4.3 convolution_convert_fusion.2
  290.0 6.5 %collective-permute-done.17 = bf16[4,64,1024]{2,1,0:T(8,128)(2,1)S(1)} collective-permute-done((bf16[4,64,1024]{2,1,0:T(8,128)(2,1)S(1)}, bf16[4,64,1024]{2,1,0:T(8,128)(2,1)S(1)}, u32[]{:S(2)}, u32[]{:S(2)}) %collective-permute-start.17) | collective-permute-done | bytes 524320 | tf_op jit(solution)/shard_map/ppermute | solution.py:33
  303.2 4.6 %pack_grad.1 = bf16[8,448,256]{2,1,0:T(8,128)(2,1)} custom-call(f32[2048,256]{1,0:T(8,128)} %fusion.21.fc1_own, bf16[2048,256]{1,0:T(8,128)(2,1)} %copy-done.31, f32[2048,192]{1,0:T(8,128)} %fusion.47.own, bf16[2048,192]{1,0:T(8,128)(2,1)} %copy.117.other), custom_call_target="tpu_custom_call" | custom-call | bytes 9000000 | tf_op jit(solution)/shard_map/pack_grad/pallas_call | solution.py:174
  307.8 13.0 %grad.1 = (bf16[8,64,1024]{2,1,0:T(8,128)(2,1)}, bf16[8,64,1024]{2,1,0:T(8,128)(2,1)}, bf16[4,2,64,1024]{3,2,1,0:T(8,128)(2,1)}, bf16[4,2,64,1024]{3,2,1,0:T(8,1...) custom-call(s32[10]{0:T(128)} %stack.155.place, ...), custom_call_target="tpu_custom_call" | custom-call | flops 3758096384 | bytes 16000000 | tf_op jit(solution)/shard_map/grad/pallas_call | solution.py:823
  340.9 8.3 %collective-permute-done.21 = bf16[2,64,1024]{2,1,0:T(8,128)(2,1)S(1)} collective-permute-done((bf16[2,64,1024]{2,1,0:T(8,128)(2,1)S(1)}, bf16[2,64,1024]{2,1,0:T(8,128)(2,1)S(1)}, u32[]{:S(2)}, u32[]{:S(2)}) %collective-permute-start.21) | collective-permute-done | bytes 262176 | tf_op jit(solution)/shard_map/ppermute | solution.py:33
  351.2 10.5 %collective-permute-done.35 = bf16[8,64,1024]{2,1,0:T(8,128)(2,1)} collective-permute-done((bf16[8,64,1024]{2,1,0:T(8,128)(2,1)}, bf16[8,64,1024]{2,1,0:T(8,128)(2,1)}, u32[]{:S(2)}, u32[]{:S(2)}) %collective-permute-start.35) | collective-permute-done | bytes 1048608 | tf_op jit(solution)/shard_map/ppermute | solution.py:33
  371.2 5.6 %collective-permute-done.36 = bf16[4,64,1024]{2,1,0:T(8,128)(2,1)S(1)} collective-permute-done((bf16[4,64,1024]{2,1,0:T(8,128)(2,1)S(1)}, bf16[4,64,1024]{2,1,0:T(8,128)(2,1)S(1)}, u32[]{:S(2)}, u32[]{:S(2)}) %collective-permute-start.36) | collective-permute-done | bytes 524320 | tf_op jit(solution)/shard_map/ppermute | solution.py:33
  377.8 3.8 all-to-all-start.3
  390.7 32.8 %collective-permute-done.39 = bf16[2,2,64,1024]{3,2,0,1:T(8,128)(2,1)} collective-permute-done((bf16[2,2,64,1024]{3,2,0,1:T(8,128)(2,1)}, bf16[2,2,64,1024]{3,2,0,1:T(8,128)(2,1)}, u32[]{:S(2)}, u32[]{:S(2)}) %collective-permute-start.39) | collective-permute-done | bytes 524320 | tf_op jit(solution)/shard_map/ppermute | solution.py:33
  431.1 6.1 %collective-permute-done.40 = bf16[2,64,1024]{2,1,0:T(8,128)(2,1)S(1)} collective-permute-done((bf16[2,64,1024]{2,1,0:T(8,128)(2,1)S(1)}, bf16[2,64,1024]{2,1,0:T(8,128)(2,1)S(1)}, u32[]{:S(2)}, u32[]{:S(2)}) %collective-permute-start.40) | collective-permute-done | bytes 262176 | tf_op jit(solution)/shard_map/ppermute | solution.py:33
  446.5 3.7 home.1
  (384 shorter events, 169.5 us)
Async XLA Ops:
  18.5 23.1 %all-to-all-start = ((bf16[8,3,128,128]{3,2,1,0:T(8,128)(2,1)}), bf16[8,3,128,128]{3,2,1,0:T(8,128)(2,1)S(1)}, u32[]{:S(2)}, u32[]{:S(2)}) async-start(bf16[8,3,128,128]{3,2,1,0:T(8,128)(2,1)} %pack.1), calls=%async_computation | async-start | bytes 1572864 | tf_op jit(solution)/shard_map/all_to_all | solution.py:37
  25.3 23.6 %collective-permute-start = (bf16[128,512]{1,0:T(8,128)(2,1)}, bf16[128,512]{1,0:T(8,128)(2,1)S(1)}, u32[]{:S(2)}, u32[]{:S(2)}) collective-permute-start(bf16[128,512]{1,0:T(8,128)(2,1)} %bitcast.12), channel_id=1, source_target_pairs={{0,1},{1,0},{2,3},{3,2},{4,5},{5,4},{6,7},{7,6},{8,9},{9,8},{10,11... | collective-permute-start | bytes 393224 | tf_op jit(solution)/shard_map/ppermute | solution.py:33
  41.5 60.8 %all-to-all-start.1 = ((bf16[8,1,256,256]{3,2,1,0:T(8,128)(2,1)}), bf16[8,1,256,256]{3,2,1,0:T(8,128)(2,1)}, u32[]{:S(2)}, u32[]{:S(2)}) async-start(bf16[8,1,256,256]{3,2,1,0:T(8,128)(2,1)} %copy.110), calls=%async_computation.1 | async-start | bytes 2097152 | tf_op jit(solution)/shard_map/all_to_all | solution.py:37
  47.6 65.8 %collective-permute-start.7 = (f32[1472]{0:T(1024)}, f32[1472]{0:T(1024)}, u32[]{:S(2)}, u32[]{:S(2)}) collective-permute-start(f32[1472]{0:T(1024)} %concatenate.174), channel_id=1, source_target_pairs={{0,1},{1,0},{2,3},{3,2},{4,5},{5,4},{6,7},{7,6},{8,9},{9,8},{10,11... | collective-permute-start | bytes 17672 | tf_op jit(solution)/shard_map/ppermute | solution.py:33
  47.6 36.2 %collective-permute-start.23 = (bf16[128,512]{1,0:T(8,128)(2,1)S(1)}, bf16[128,512]{1,0:T(8,128)(2,1)S(1)}, u32[]{:S(2)}, u32[]{:S(2)}) collective-permute-start(bf16[128,512]{1,0:T(8,128)(2,1)S(1)} %bitcast.266), channel_id=1, source_target_pairs={{0,1},{1,0},{2,3},{3,2},{4,5},{5,4},{6,7},{7,6},{8,9},{9,8},{10,11... | collective-permute-start | bytes 393224 | tf_op jit(solution)/shard_map/ppermute | solution.py:33
  49.0 32.0 %collective-permute-start.1 = (bf16[2,64,1024]{2,1,0:T(8,128)(2,1)S(1)}, bf16[2,64,1024]{2,1,0:T(8,128)(2,1)S(1)}, u32[]{:S(2)}, u32[]{:S(2)}) collective-permute-start(bf16[2,64,1024]{2,1,0:T(8,128)(2,1)S(1)} %maximum_select_fusion.3), channel_id=1, source_target_pairs={{0,16},{16,0},{1,17},{17,1},{2,18},{18,2},{3,19},{19,3},{4,20},{20... | collective-permute-start | bytes 786440 | tf_op jit(solution)/shard_map/ppermute | solution.py:33
  82.0 19.2 %collective-permute-start.2 = (bf16[2,2,64,1024]{3,2,0,1:T(8,128)(2,1)}, bf16[2,2,64,1024]{3,2,0,1:T(8,128)(2,1)}, u32[]{:S(2)}, u32[]{:S(2)}) collective-permute-start(bf16[2,2,64,1024]{3,2,0,1:T(8,128)(2,1)} %pad_maximum_fusion.9), channel_id=1, source_target_pairs={{0,8},{8,0},{1,9},{9,1},{2,10},{10,2},{3,11},{11,3},{4,12},{12,4},... | collective-permute-start | bytes 1572872 | tf_op jit(solution)/shard_map/ppermute | solution.py:33
  98.1 18.6 %collective-permute-start.25 = (bf16[2,2,64,1024]{3,2,1,0:T(8,128)(2,1)}, bf16[2,2,64,1024]{3,2,1,0:T(8,128)(2,1)}, u32[]{:S(2)}, u32[]{:S(2)}) collective-permute-start(bf16[2,2,64,1024]{3,2,1,0:T(8,128)(2,1)} %pad_maximum_fusion.11), channel_id=1, source_target_pairs={{0,8},{8,0},{1,9},{9,1},{2,10},{10,2},{3,11},{11,3},{4,12},{12,4},... | collective-permute-start | bytes 1572872 | tf_op jit(solution)/shard_map/ppermute | solution.py:33
  102.4 64.4 %all-to-all-start.2 = ((bf16[8,1,320,256]{3,2,1,0:T(8,128)(2,1)}), bf16[8,1,320,256]{3,2,1,0:T(8,128)(2,1)S(1)}, u32[]{:S(2)}, u32[]{:S(2)}) async-start(bf16[8,1,320,256]{3,2,1,0:T(8,128)(2,1)} %maximum_bitcast_fusion), calls=%async_computation.2 | async-start | bytes 2621440 | tf_op jit(solution)/shard_map/all_to_all | solution.py:37
  114.7 22.0 %collective-permute-start.3 = (bf16[4,64,1024]{2,1,0:T(8,128)(2,1)}, bf16[4,64,1024]{2,1,0:T(8,128)(2,1)S(1)}, u32[]{:S(2)}, u32[]{:S(2)}) collective-permute-start(bf16[4,64,1024]{2,1,0:T(8,128)(2,1)} %get-tuple-element.115), channel_id=1, source_target_pairs={{0,4},{4,0},{1,5},{5,1},{2,6},{6,2},{3,7},{7,3},{8,12},{12,8},{9,1... | collective-permute-start | bytes 1572872 | tf_op jit(solution)/shard_map/ppermute | solution.py:33
  119.3 38.8 %collective-permute-start.26 = (bf16[4,64,1024]{2,1,0:T(8,128)(2,1)}, bf16[4,64,1024]{2,1,0:T(8,128)(2,1)}, u32[]{:S(2)}, u32[]{:S(2)}) collective-permute-start(bf16[4,64,1024]{2,1,0:T(8,128)(2,1)} %get-tuple-element.111), channel_id=1, source_target_pairs={{0,4},{4,0},{1,5},{5,1},{2,6},{6,2},{3,7},{7,3},{8,12},{12,8},{9,1... | collective-permute-start | bytes 1572872 | tf_op jit(solution)/shard_map/ppermute | solution.py:33
  126.8 42.0 %collective-permute-start.6 = (bf16[2,4,64,1024]{3,2,1,0:T(8,128)(2,1)}, bf16[2,4,64,1024]{3,2,1,0:T(8,128)(2,1)}, u32[]{:S(2)}, u32[]{:S(2)}) collective-permute-start(bf16[2,4,64,1024]{3,2,1,0:T(8,128)(2,1)} %pad_maximum_fusion.3.seconds), channel_id=1, source_target_pairs={{0,4},{4,0},{1,5},{5,1},{2,6},{6,2},{3,7},{7,3},{8,12},{12,8},{9,1... | collective-permute-start | bytes 3145736 | tf_op jit(solution)/shard_map/ppermute | solution.py:33
  137.9 30.9 %collective-permute-start.4 = (bf16[2,4,64,1024]{3,2,1,0:T(8,128)(2,1)}, bf16[2,4,64,1024]{3,2,1,0:T(8,128)(2,1)}, u32[]{:S(2)}, u32[]{:S(2)}) collective-permute-start(bf16[2,4,64,1024]{3,2,1,0:T(8,128)(2,1)} %pad_maximum_fusion.2.firsts), channel_id=1, source_target_pairs={{0,2},{2,0},{1,3},{3,1},{4,6},{6,4},{5,7},{7,5},{8,10},{10,8},{9,1... | collective-permute-start | bytes 3145736 | tf_op jit(solution)/shard_map/ppermute | solution.py:33
  138.4 30.4 %collective-permute-start.13 = (bf16[2048,256]{1,0:T(8,128)(2,1)}, bf16[2048,256]{1,0:T(8,128)(2,1)}, u32[]{:S(2)}, u32[]{:S(2)}) collective-permute-start(bf16[2048,256]{1,0:T(8,128)(2,1)} %bitcast.34.fc1_own), channel_id=1, source_target_pairs={{0,1},{1,0},{2,3},{3,2},{4,5},{5,4},{6,7},{7,6},{8,9},{9,8},{10,11... | collective-permute-start | bytes 3145736 | tf_op jit(solution)/shard_map/ppermute | solution.py:33
  138.4 19.6 %collective-permute-start.8 = (f32[2,1024]{1,0:T(2,128)S(1)}, f32[2,1024]{1,0:T(2,128)S(1)}, u32[]{:S(2)}, u32[]{:S(2)}) collective-permute-start(f32[2,1024]{1,0:T(2,128)S(1)} %maximum_select_fusion.9), channel_id=1, source_target_pairs={{0,2},{2,0},{1,3},{3,1},{4,6},{6,4},{5,7},{7,5},{8,10},{10,8},{9,1... | collective-permute-start | bytes 24584 | tf_op jit(solution)/shard_map/ppermute | solution.py:33
  158.0 24.4 %collective-permute-start.28 = (bf16[4,64,1024]{2,1,0:T(8,128)(2,1)}, bf16[4,64,1024]{2,1,0:T(8,128)(2,1)}, u32[]{:S(2)}, u32[]{:S(2)}) collective-permute-start(bf16[4,64,1024]{2,1,0:T(8,128)(2,1)} %get-tuple-element.112), channel_id=1, source_target_pairs={{0,2},{2,0},{1,3},{3,1},{4,6},{6,4},{5,7},{7,5},{8,10},{10,8},{9,1... | collective-permute-start | bytes 1572872 | tf_op jit(solution)/shard_map/ppermute | solution.py:33
  163.1 41.9 %collective-permute-start.27 = (bf16[2,4,64,1024]{3,2,1,0:T(8,128)(2,1)}, bf16[2,4,64,1024]{3,2,1,0:T(8,128)(2,1)}, u32[]{:S(2)}, u32[]{:S(2)}) collective-permute-start(bf16[2,4,64,1024]{3,2,1,0:T(8,128)(2,1)} %pad_maximum_fusion.5.firsts), channel_id=1, source_target_pairs={{0,2},{2,0},{1,3},{3,1},{4,6},{6,4},{5,7},{7,5},{8,10},{10,8},{9,1... | collective-permute-start | bytes 3145736 | tf_op jit(solution)/shard_map/ppermute | solution.py:33
  168.8 34.3 %collective-permute-start.15 = (bf16[8,320,256]{2,1,0:T(8,128)(2,1)S(1)}, bf16[8,320,256]{2,1,0:T(8,128)(2,1)S(1)}, u32[]{:S(2)}, u32[]{:S(2)}) collective-permute-start(bf16[8,320,256]{2,1,0:T(8,128)(2,1)S(1)} %bitcast.230), channel_id=1, source_target_pairs={{0,1},{1,0},{2,3},{3,2},{4,5},{5,4},{6,7},{7,6},{8,9},{9,8},{10,11... | collective-permute-start | bytes 3932168 | tf_op jit(solution)/shard_map/ppermute | solution.py:33
  184.6 25.4 %collective-permute-start.29 = (bf16[2,4,64,1024]{3,2,1,0:T(8,128)(2,1)}, bf16[2,4,64,1024]{3,2,1,0:T(8,128)(2,1)}, u32[]{:S(2)}, u32[]{:S(2)}) collective-permute-start(bf16[2,4,64,1024]{3,2,1,0:T(8,128)(2,1)} %pad_maximum_fusion.6.seconds), channel_id=1, source_target_pairs={{0,4},{4,0},{1,5},{5,1},{2,6},{6,2},{3,7},{7,3},{8,12},{12,8},{9,1... | collective-permute-start | bytes 3145736 | tf_op jit(solution)/shard_map/ppermute | solution.py:33
  226.7 24.0 %collective-permute-start.32 = (bf16[2048,256]{1,0:T(8,128)(2,1)}, bf16[2048,256]{1,0:T(8,128)(2,1)S(1)}, u32[]{:S(2)}, u32[]{:S(2)}) collective-permute-start(bf16[2048,256]{1,0:T(8,128)(2,1)} %convolution_convert_fusion), channel_id=1, source_target_pairs={{0,1},{1,0},{2,3},{3,2},{4,5},{5,4},{6,7},{7,6},{8,9},{9,8},{10,11... | collective-permute-start | bytes 3145736 | tf_op jit(solution)/shard_map/ppermute | solution.py:33
  240.8 27.5 %collective-permute-start.16 = (bf16[8,64,1024]{2,1,0:T(8,128)(2,1)}, bf16[8,64,1024]{2,1,0:T(8,128)(2,1)S(1)}, u32[]{:S(2)}, u32[]{:S(2)}) collective-permute-start(bf16[8,64,1024]{2,1,0:T(8,128)(2,1)} %get-tuple-element.71), channel_id=1, source_target_pairs={{0,2},{2,0},{1,3},{3,1},{4,6},{6,4},{5,7},{7,5},{8,10},{10,8},{9,1... | collective-permute-start | bytes 3145736 | tf_op jit(solution)/shard_map/ppermute | solution.py:33
  241.8 31.6 %collective-permute-start.18 = (bf16[4,2,64,1024]{3,2,1,0:T(8,128)(2,1)}, bf16[4,2,64,1024]{3,2,1,0:T(8,128)(2,1)}, u32[]{:S(2)}, u32[]{:S(2)}) collective-permute-start(bf16[4,2,64,1024]{3,2,1,0:T(8,128)(2,1)} %get-tuple-element.73), channel_id=1, source_target_pairs={{0,4},{4,0},{1,5},{5,1},{2,6},{6,2},{3,7},{7,3},{8,12},{12,8},{9,1... | collective-permute-start | bytes 3145736 | tf_op jit(solution)/shard_map/ppermute | solution.py:33
  263.2 114.5 %all-to-all-start.4 = ((bf16[8,1,320,256]{3,2,1,0:T(8,128)(2,1)}), bf16[8,1,320,256]{3,2,1,0:T(8,128)(2,1)S(1)}, u32[]{:S(2)}, u32[]{:S(2)}) async-start(bf16[8,1,320,256]{3,2,1,0:T(8,128)(2,1)} %pad_maximum_fusion), calls=%async_computation.4 | async-start | bytes 2621440 | tf_op jit(solution)/shard_map/all_to_all | solution.py:37
  271.3 25.2 %collective-permute-start.17 = (bf16[4,64,1024]{2,1,0:T(8,128)(2,1)S(1)}, bf16[4,64,1024]{2,1,0:T(8,128)(2,1)S(1)}, u32[]{:S(2)}, u32[]{:S(2)}) collective-permute-start(bf16[4,64,1024]{2,1,0:T(8,128)(2,1)S(1)} %slice.370), channel_id=1, source_target_pairs={{0,4},{4,0},{1,5},{5,1},{2,6},{6,2},{3,7},{7,3},{8,12},{12,8},{9,1... | collective-permute-start | bytes 1572872 | tf_op jit(solution)/shard_map/ppermute | solution.py:33
  276.7 19.9 %collective-permute-start.19 = (bf16[4,64,1024]{2,1,0:T(8,128)(2,1)}, bf16[4,64,1024]{2,1,0:T(8,128)(2,1)}, u32[]{:S(2)}, u32[]{:S(2)}) collective-permute-start(bf16[4,64,1024]{2,1,0:T(8,128)(2,1)} %slice_bitcast_fusion.2), channel_id=1, source_target_pairs={{0,2},{2,0},{1,3},{3,1},{4,6},{6,4},{5,7},{7,5},{8,10},{10,8},{9,1... | collective-permute-start | bytes 1572872 | tf_op jit(solution)/shard_map/ppermute | solution.py:33
  298.1 27.2 %collective-permute-start.20 = (bf16[2,2,64,1024]{3,2,0,1:T(8,128)(2,1)S(1)}, bf16[2,2,64,1024]{3,2,0,1:T(8,128)(2,1)S(1)}, u32[]{:S(2)}, u32[]{:S(2)}) collective-permute-start(bf16[2,2,64,1024]{3,2,0,1:T(8,128)(2,1)S(1)} %pad_maximum_fusion.8), channel_id=1, source_target_pairs={{0,8},{8,0},{1,9},{9,1},{2,10},{10,2},{3,11},{11,3},{4,12},{12,4},... | collective-permute-start | bytes 1572872 | tf_op jit(solution)/shard_map/ppermute | solution.py:33
  336.5 25.3 %collective-permute-start.35 = (bf16[8,64,1024]{2,1,0:T(8,128)(2,1)}, bf16[8,64,1024]{2,1,0:T(8,128)(2,1)}, u32[]{:S(2)}, u32[]{:S(2)}) collective-permute-start(bf16[8,64,1024]{2,1,0:T(8,128)(2,1)} %get-tuple-element.94), channel_id=1, source_target_pairs={{0,2},{2,0},{1,3},{3,1},{4,6},{6,4},{5,7},{7,5},{8,10},{10,8},{9,1... | collective-permute-start | bytes 3145736 | tf_op jit(solution)/shard_map/ppermute | solution.py:33
  337.0 28.7 %collective-permute-start.37 = (bf16[4,2,64,1024]{3,2,1,0:T(8,128)(2,1)}, bf16[4,2,64,1024]{3,2,1,0:T(8,128)(2,1)}, u32[]{:S(2)}, u32[]{:S(2)}) collective-permute-start(bf16[4,2,64,1024]{3,2,1,0:T(8,128)(2,1)} %get-tuple-element.96), channel_id=1, source_target_pairs={{0,4},{4,0},{1,5},{5,1},{2,6},{6,2},{3,7},{7,3},{8,12},{12,8},{9,1... | collective-permute-start | bytes 3145736 | tf_op jit(solution)/shard_map/ppermute | solution.py:33
  351.2 19.4 %collective-permute-start.45 = (f32[5376]{0:T(1024)S(1)}, f32[5376]{0:T(1024)S(1)}, u32[]{:S(2)}, u32[]{:S(2)}) collective-permute-start(f32[5376]{0:T(1024)S(1)} %pad_maximum_fusion.14), channel_id=1, source_target_pairs={{0,16},{16,0},{1,17},{17,1},{2,18},{18,2},{3,19},{19,3},{4,20},{20... | collective-permute-start | bytes 64520 | tf_op jit(solution)/shard_map/ppermute | solution.py:33
  369.8 57.5 %collective-permute-start.22 = (f32[128,512]{1,0:T(8,128)}, f32[128,512]{1,0:T(8,128)}, u32[]{:S(2)}, u32[]{:S(2)}) collective-permute-start(f32[128,512]{1,0:T(8,128)} %bitcast.224), channel_id=1, source_target_pairs={{0,1},{1,0},{2,3},{3,2},{4,5},{5,4},{6,7},{7,6},{8,9},{9,8},{10,11... | collective-permute-start | bytes 786440 | tf_op jit(solution)/shard_map/ppermute | solution.py:33
  377.8 67.5 %all-to-all-start.3 = ((bf16[8,448,256]{2,1,0:T(8,128)(2,1)}), bf16[8,448,256]{2,1,0:T(8,128)(2,1)S(1)}, u32[]{:S(2)}, u32[]{:S(2)}) async-start(bf16[8,448,256]{2,1,0:T(8,128)(2,1)} %pack_grad.1), calls=%async_computation.3 | async-start | bytes 3670016 | tf_op jit(solution)/shard_map/all_to_all | solution.py:37
  385.6 37.8 %collective-permute-start.39 = (bf16[2,2,64,1024]{3,2,0,1:T(8,128)(2,1)}, bf16[2,2,64,1024]{3,2,0,1:T(8,128)(2,1)}, u32[]{:S(2)}, u32[]{:S(2)}) collective-permute-start(bf16[2,2,64,1024]{3,2,0,1:T(8,128)(2,1)} %pad_maximum_fusion.7), channel_id=1, source_target_pairs={{0,8},{8,0},{1,9},{9,1},{2,10},{10,2},{3,11},{11,3},{4,12},{12,4},... | collective-permute-start | bytes 1572872 | tf_op jit(solution)/shard_map/ppermute | solution.py:33
  (85 other events, 1121.9 us)
where the time goes:
time: 456 us; the launch traced here: 451 us
  waiting for transfers between devices  163 us (36%)
  Pallas kernels  83.6 us (18%)
  starting transfers between devices  74.1 us (16%)
  other arithmetic  55.5 us (12%)
  local copies, waits for them, and re-layouts  49.9 us (11%)
  matrix products  23.6 us (5%)
    ppermute x47, waiting for transfers between devices, swap(): return lax.ppermute(values, axis, [(0, 1), (1, 0)])  148 us
    ppermute x47, starting transfers between devices, swap(): return lax.ppermute(values, axis, [(0, 1), (1, 0)])  50.1 us
    all_to_all x5, starting transfers between devices, spread(): return lax.all_to_all(pieces, LOX, 0, 0, tiled=True)  24 us
    dot_general x8, matrix products, dot(): lax.dot_general(left, right, (((left_dim,), (right_dim,)), ((), ())), pre...  23.6 us
    all_to_all x5, waiting for transfers between devices, spread(): return lax.all_to_all(pieces, LOX, 0, 0, tiled=True)  14.4 us
    pallas_call x1, Pallas kernels, front(): pl.pallas_call(front_kernel, grid=(tokens // STEP,), out_shape=(shape(D,...  13.1 us
    pallas_call x1, Pallas kernels, grad_units(): pl.pallas_call(grad_kernel, grid=(tokens // STEP,), out_shape=(*partial_s...  13 us
    pallas_call x1, Pallas kernels, attend_back(): pl.pallas_call(functools.partial(attend_back_kernel, tiles, blocks), out_...  12.4 us
  transfers between devices with their start and end apart: 52, of which 18 were waited for; matrix products, arithmetic and copies ran while one was open for 25% of the time, Pallas kernels for 15%

commit v1 on v0

--- a/solution.py
+++ b/solution.py
@@ -17,6 +17,7 @@
 LO = 8
 UNIT = 1024
 STEP = 256
+IDS = 16
 
 epsilon = 1e-05
 cubic_coef = 0.044715
@@ -42,10 +43,13 @@
     pair = jnp.stack([unit, swap(unit, "zh")])
     quad = jnp.concatenate([pair, swap(pair, "zl")])
     first, second = quad[:, 0], quad[:, 1]
-    firsts = jnp.stack([first, swap(first, "x")])
-    seconds = jnp.stack([second, swap(second, "y")])
-    firsts_y = swap(firsts, "y")
-    return firsts, firsts_y, seconds, swap(seconds, "x")
+    first_x = swap(first, "x")
+    second_y = swap(second, "y")
+    first_y = swap(first, "y")
+    second_x = swap(second, "x")
+    first_xy = swap(first_x, "y")
+    second_yx = swap(second_y, "x")
+    return first, first_x, first_y, first_xy, second, second_x, second_y, second_yx
 
 
 def scatter_pieces(a_own, a_other, b_near, b_far):
@@ -87,21 +91,20 @@
     return pl.BlockSpec(memory_space=pltpu.SMEM)
 
 
+PIECES = 8
+
+
 def piece_specs():
-    near = pl.BlockSpec((1, 2, HALF, UNIT), lambda i: (i // 2, i % 2, 0, 0))
-    both = pl.BlockSpec((2, 2, HALF, UNIT), lambda i: (0, i % 2, 0, 0))
-    return [near, near, both, both]
-
-
-def piece_rows(step, firsts, firsts_y, seconds, seconds_x):
-    later = jnp.where(step < 2, seconds[...], seconds_x[...])
-    sides = []
-    for side, first in enumerate((firsts, firsts_y)):
-        parts = []
-        for s in range(2):
-            parts += [first[0, s], later[side, s]]
-        sides.append(jnp.concatenate(parts, axis=0))
-    return sides
+    return [pl.BlockSpec((2, HALF, UNIT), lambda i: (i % 2, 0, 0)) for _ in range(PIECES)]
+
+
+def piece_rows(step, pieces):
+    near = step < 2
+    chosen = [jnp.where(near, pieces[i][...], pieces[i + 1][...]) for i in (0, 2, 4, 6)]
+    return [
+        jnp.concatenate([first[0], second[0], first[1], second[1]], axis=0)
+        for first, second in ((chosen[0], chosen[2]), (chosen[1], chosen[3]))
+    ]
 
 
 def sides_of(place):
@@ -112,24 +115,25 @@
     ]
 
 
-def pack_kernel(weight, out):
+def pack_kernel(weight, ids, out):
     for c in range(LO):
+        out[c, 3 * BLK :] = ids[...]
         columns = slice(c * HD, (c + 1) * HD)
         for j in range(3):
-            out[c, j] = jnp.concatenate(
+            out[c, j * BLK : (j + 1) * BLK] = jnp.concatenate(
                 [weight[j, :BLK, columns], weight[j, BLK:, columns]], axis=1
             )
 
 
-def pack_heads(weight):
+def pack_heads(weight, ids):
     return pl.pallas_call(
         pack_kernel,
-        out_shape=jax.ShapeDtypeStruct((LO, 3, BLK, BLK), BF),
-        in_specs=full_spec(1),
+        out_shape=jax.ShapeDtypeStruct((LO, 3 * BLK + IDS, BLK), BF),
+        in_specs=full_spec(2),
         out_specs=full_spec(1)[0],
         cost_estimate=cost(0, 1600000),
         name="pack",
-    )(weight)
+    )(weight, ids)
 
 
 def join_kernel(own, other, out):
@@ -139,7 +143,11 @@
             rows = pl.ds(c * 2 * BLK + u * BLK, BLK)
             for j in range(3):
                 out[rows, j * BLK : (j + 1) * BLK] = jnp.concatenate(
-                    [own[c, j, :, columns], other[c, j, :, columns]], axis=1
+                    [
+                        half[c, j * BLK : (j + 1) * BLK, columns]
+                        for half in (own, other)
+                    ],
+                    axis=1,
                 )
 
 
@@ -473,12 +481,13 @@
     )(table, q, k_own, v_own, k_other, v_other, cot, att, log_in)
 
 
-def front_kernel(
+def front_kernel(place, *refs):
+    front_body(place, refs[:PIECES], *refs[PIECES:])
+
+
+def front_body(
     place,
-    firsts,
-    firsts_y,
-    seconds,
-    seconds_x,
+    pieces,
     gain,
     shift,
     qkv,
@@ -502,7 +511,7 @@
     sides = sides_of(place)
     rows = [
         part.astype(F32)
-        for part in piece_rows(pl.program_id(0), firsts, firsts_y, seconds, seconds_x)
+        for part in piece_rows(pl.program_id(0), pieces)
     ]
     center = sum(jnp.sum(part, axis=-1, keepdims=True) for part in rows) / D
     rows = [part - center for part in rows]
@@ -625,25 +634,30 @@
     )
 
 
-def mix_kernel(place, attended, active, out2, fc2_own, fc2_other, *partial):
-    hidden = fc2_own.shape[1]
+def out_rows(c, down_own, down_other):
+    hidden = down_own.shape[1] - HD
+    return jnp.concatenate([down_own[c, hidden:], down_other[c, hidden:]], axis=0)
+
+
+def mix_kernel(place, attended, active, down_own, down_other, *partial):
+    hidden = down_own.shape[1] - HD
     for index, side in enumerate((place[0], 1 - place[0])):
         parts = []
         for quarter in range(4):
             c = 4 * side + quarter
             parts.append(
                 (
-                    dot(active[:, :hidden], fc2_own[c], 1, 0)
-                    + dot(active[:, hidden:], fc2_other[c], 1, 0)
-                    + dot(attended[...], out2[c], 1, 0)
+                    dot(active[:, :hidden], down_own[c, :hidden], 1, 0)
+                    + dot(active[:, hidden:], down_other[c, :hidden], 1, 0)
+                    + dot(attended[...], out_rows(c, down_own, down_other), 1, 0)
                 ).astype(BF)
             )
         store_pieces(pl.program_id(0), index, jnp.concatenate(parts, axis=1), *partial)
 
 
-def mix(place, attended, active, out2, fc2_own, fc2_other):
+def mix(place, attended, active, down_own, down_other):
     tokens = LO * BLK
-    hidden = fc2_own.shape[1]
+    hidden = down_own.shape[1] - HD
     return pl.pallas_call(
         mix_kernel,
         grid=(tokens // STEP,),
@@ -652,26 +666,25 @@
             scalar_spec(),
             rows_spec(BLK),
             rows_spec(2 * hidden),
-            fixed_spec(LO, BLK, 256),
-            fixed_spec(LO, hidden, 256),
-            fixed_spec(LO, hidden, 256),
+            fixed_spec(LO, hidden + HD, 256),
+            fixed_spec(LO, hidden + HD, 256),
         ],
         out_specs=partial_specs(),
         cost_estimate=cost(2 * tokens * D * (128 + 2 * hidden), 8000000),
         name="mix",
-    )(place, attended, active, out2, fc2_own, fc2_other)
-
-
-def back_kernel(
+    )(place, attended, active, down_own, down_other)
+
+
+def back_kernel(place, *refs):
+    back_body(place, refs[:PIECES], *refs[PIECES:])
+
+
+def back_body(
     place,
-    firsts,
-    firsts_y,
-    seconds,
-    seconds_x,
+    pieces,
     pre,
-    out2,
-    fc2_own,
-    fc2_other,
+    down_own,
+    down_other,
     cot,
     grad_pre,
     grad_attended,
@@ -681,34 +694,34 @@
     def _():
         bias_sum[...] = jnp.zeros_like(bias_sum)
 
-    parts = piece_rows(pl.program_id(0), firsts, firsts_y, seconds, seconds_x)
+    parts = piece_rows(pl.program_id(0), pieces)
     for part, side in zip(parts, sides_of(place)):
         cot[:, side] = part
     rows = cot[...]
-    hidden = fc2_own.shape[1]
+    hidden = down_own.shape[1] - HD
 
     def through(weight):
         total = 0.0
         for c in range(LO):
-            total = total + dot(rows[:, c * 256 : (c + 1) * 256], weight[c], 1, 1)
+            total = total + dot(rows[:, c * 256 : (c + 1) * 256], weight(c), 1, 1)
         return total
 
-    grad_attended[...] = through(out2).astype(BF)
-    for part, weight in enumerate((fc2_own, fc2_other)):
+    grad_attended[...] = through(lambda c: out_rows(c, down_own, down_other)).astype(BF)
+    for part, weight in enumerate((down_own, down_other)):
         columns = slice(part * hidden, (part + 1) * hidden)
         value = pre[:, columns]
         inner = jnp.tanh(inner_coef * (value + cubic_coef * value * value * value))
         slope = 0.5 * (1.0 + inner) + 0.5 * value * (1.0 - inner * inner) * inner_coef * (
             1.0 + 3.0 * cubic_coef * value * value
         )
-        grad = through(weight) * slope
+        grad = through(lambda c: weight[c, :hidden]) * slope
         bias_sum[:, columns] += jnp.sum(grad, axis=0, keepdims=True)
         grad_pre[:, columns] = grad.astype(BF)
 
 
-def back(place, pieces, pre, out2, fc2_own, fc2_other):
+def back(place, pieces, pre, down_own, down_other):
     tokens = LO * BLK
-    hidden = fc2_own.shape[1]
+    hidden = down_own.shape[1] - HD
     return pl.pallas_call(
         back_kernel,
         grid=(tokens // STEP,),
@@ -722,9 +735,8 @@
             scalar_spec(),
             *piece_specs(),
             rows_spec(2 * hidden),
-            fixed_spec(LO, BLK, 256),
-            fixed_spec(LO, hidden, 256),
-            fixed_spec(LO, hidden, 256),
+            fixed_spec(LO, hidden + HD, 256),
+            fixed_spec(LO, hidden + HD, 256),
         ],
         out_specs=(
             rows_spec(D),
@@ -734,7 +746,7 @@
         ),
         cost_estimate=cost(2 * tokens * D * (128 + 2 * hidden), 14000000),
         name="back",
-    )(place, *pieces, pre, out2, fc2_own, fc2_other)
+    )(place, *pieces, pre, down_own, down_other)
 
 
 def unturn_kernel(dq, dk, dv, got, cosine, sine_a, sine_b, joint, own, other, bias):
@@ -767,12 +779,13 @@
     )(dq, dk, dv, got, cosine, sine_a, sine_b)
 
 
-def grad_kernel(
+def grad_kernel(place, *refs):
+    grad_body(place, refs[:PIECES], *refs[PIECES:])
+
+
+def grad_body(
     place,
-    firsts,
-    firsts_y,
-    seconds,
-    seconds_x,
+    pieces,
     mean,
     inv,
     gain,
@@ -797,7 +810,7 @@
         shift_sum[...] = jnp.zeros_like(shift_sum)
 
     hidden = fc1_own.shape[1]
-    parts = piece_rows(step, firsts, firsts_y, seconds, seconds_x)
+    parts = piece_rows(step, pieces)
     first, second = 0.0, 0.0
     for index, (side, part) in enumerate(zip(sides_of(place), parts)):
         grads = (
@@ -896,10 +909,6 @@
     pieces = gather_pieces(unit_in)
     unit_cot = make_unit(grad_output)
     pieces_cot = gather_pieces(unit_cot)
-    ids = half(position_ids, k)
-    for name in ("zh", "zl", "x"):
-        ids = jnp.stack([ids, swap(ids, name)])
-    ids, w_fc1, w_qkv, w_fc2, w_out = lax.optimization_barrier((ids, w_fc1, w_qkv, w_fc2, w_out))
     slot_lo = [lo ^ (((s & 1) << 2) | (s & 2) | (s >> 2)) for s in range(LO)]
     place = jnp.stack([y, k] + slot_lo).astype(jnp.int32)
 
@@ -921,12 +930,19 @@
     else:
         down_own = down.transpose(2, 1, 0, 3).reshape(hidden + HD, LO, 256).transpose(1, 0, 2)
     down_other = swap(down_own, "k")
-    fc2_own, fc2_other = down_own[:, :hidden], down_other[:, :hidden]
-    out2 = jnp.concatenate([down_own[:, hidden:], down_other[:, hidden:]], axis=1)
     if n_hi == 1:
-        heads_own = spread(pack_heads(w_qkv.transpose(1, 0, 2)))
+        ids = half(position_ids, k)
+        ids = jnp.stack([ids // BLK, ids % BLK]).astype(BF)
+        ids = jnp.concatenate([ids, jnp.zeros((IDS - 2, BLK), BF)])
+        heads_own = spread(pack_heads(w_qkv.transpose(1, 0, 2), ids))
         qkv = join_heads(heads_own, swap(heads_own, "k"))
+        ids = heads_own[:, 3 * BLK : 3 * BLK + 2].astype(jnp.int32)
+        ids = ids[:, 0] * BLK + ids[:, 1]
+        ids = jnp.stack([lax.dynamic_index_in_dim(ids, c, 0, keepdims=False) for c in slot_lo])
     else:
+        ids = half(position_ids, k)
+        for name in ("zh", "zl", "x"):
+            ids = jnp.stack([ids, swap(ids, name)])
         cut = over_hi(w_qkv).reshape(n_hi, depth, 3, LO, HD).transpose(3, 0, 1, 2, 4)
         heads_own = spread(cut.reshape(LO, n_hi, depth, 3 * HD))
         heads_own = ordered(heads_own, (D, 3, HD))
@@ -990,9 +1006,11 @@
 
     key_set = tuple(all_keys(v) for v in (keys, values, other_kv[0], other_kv[1]))
     attended, log_total = attend(tiles, blocks, table, queries, *key_set)
-    summed = scatter_pieces(*mix(place, attended, active, out2, fc2_own, fc2_other))
-
-    cot, grad_pre, grad_attended, term_bias1 = back(place, pieces_cot, pre, out2, fc2_own, fc2_other)
+    summed = scatter_pieces(*mix(place, attended, active, down_own, down_other))
+
+    cot, grad_pre, grad_attended, term_bias1 = back(
+        place, pieces_cot, pre, down_own, down_other
+    )
 
     def summed_dot(left, own, other, flip):
         def product(right):
@@ -1016,11 +1034,8 @@
     fc2_sum = add(*summed_dot(cot, active[:, :hidden], active[:, hidden:], True))
     out_sum = add(*summed_dot(cot, attended[:, :HD], attended[:, HD:], True))
     down = jnp.concatenate([cut_columns(fc2_sum), cut_columns(out_sum)], axis=2)
-    fc1_term, fc1_got = summed_dot(normed16, grad_pre[:, :hidden], grad_pre[:, hidden:], False)
     if n_hi == 1:
-        grad_attended, down, fc1_term, fc1_got = lax.optimization_barrier(
-            (grad_attended, down, fc1_term, fc1_got)
-        )
+        grad_attended, down = lax.optimization_barrier((grad_attended, down))
     down_home = home(down)
     grad_fc2 = down_home[:, :hidden].reshape(LO * hidden, depth).astype(F32)
     grad_out = down_home[:, hidden:].reshape(LO * HD, depth).astype(F32)
@@ -1042,10 +1057,17 @@
     joint, joint_own, joint_other, term_joint_bias = unturn(
         dq, dk, dv, got, cosine, sine_a, sine_b
     )
-    own_term, got_term = summed_dot(normed16, joint_own, joint_other, False)
+    *partial, row_sums, gain_sum, shift_sum = grad_units(
+        place, pieces, mean, inv, gain, joint, grad_pre, qkv, fc1_own, fc1_other
+    )
+    if n_hi == 1:
+        late, *partial = lax.optimization_barrier((normed16, *partial))
+    else:
+        late = normed16
+    fc1_term, fc1_got = summed_dot(late, grad_pre[:, :hidden], grad_pre[:, hidden:], False)
+    own_term, got_term = summed_dot(late, joint_own, joint_other, False)
     if n_hi == 1:
         packed = pack_grads(fc1_term, fc1_got, own_term, got_term)
-        packed, joint = lax.optimization_barrier((packed, joint))
         grad_fc1, grad_qkv = home_grads(spread(packed))
         grad_qkv = grad_qkv.transpose(1, 0, 2)
     else:
@@ -1055,9 +1077,6 @@
         qkv_sum = add(own_term, got_term).reshape(n_hi, LO, depth, 3 * HD)
         qkv_home = home(qkv_sum.transpose(1, 0, 2, 3)).reshape(LO, depth, 3, HD)
         grad_qkv = qkv_home.transpose(1, 2, 0, 3).reshape(depth, 3, width).astype(F32)
-    *partial, row_sums, gain_sum, shift_sum = grad_units(
-        place, pieces, mean, inv, gain, joint, grad_pre, qkv, fc1_own, fc1_other
-    )
     grad_unit = scatter_pieces(*partial)
 
     heads = lax.dynamic_update_slice(

time: 456 us -> 418 us (0.917)
  other arithmetic: 55.5 us -> 41.7 us
  starting transfers between devices: 74.1 us -> 64.9 us
  waiting for transfers between devices: 163 us -> 154 us
  local copies, waits for them, and re-layouts: 49.9 us -> 42.2 us
    ppermute x47 -> x48, waiting for transfers between devices: 148 us -> 137 us  [swap(): return lax.ppermute(values, axis, [(0, 1), (1, 0)])]
    ppermute x47 -> x48, starting transfers between devices: 50.1 us -> 41.4 us  [swap(): return lax.ppermute(values, axis, [(0, 1), (1, 0)])]
    another operation x7 -> x2, other arithmetic: 8.14 us -> 0.62 us  [the longest x1 0.6 us: step_body(): ids = jnp.stack([ids // BLK, ids % BLK]).astype(BF)]
    unnamed x145 -> x154, local copies, waits for them, and re-layouts: 9.04 us -> 11.8 us
  transfers between devices with their start and end apart: 52 -> 53, of which waited for: 18 -> 21; matrix products, arithmetic and copies ran while one was open for 25% -> 22% of each run, Pallas kernels for 15% -> 17%
where the time goes in v1:
time: 418 us; the launch traced here: 414 us
  waiting for transfers between devices  154 us (37%)
  Pallas kernels  85.5 us (20%)
  starting transfers between devices  64.9 us (16%)
  local copies, waits for them, and re-layouts  42.2 us (10%)
  other arithmetic  41.7 us (10%)
  matrix products  23.3 us (6%)
    ppermute x48, waiting for transfers between devices, swap(): return lax.ppermute(values, axis, [(0, 1), (1, 0)])  137 us
    ppermute x48, starting transfers between devices, swap(): return lax.ppermute(values, axis, [(0, 1), (1, 0)])  41.4 us
    all_to_all x5, starting transfers between devices, spread(): return lax.all_to_all(pieces, LOX, 0, 0, tiled=True)  23.5 us
    dot_general x8, matrix products, dot(): lax.dot_general(left, right, (((left_dim,), (right_dim,)), ((), ())), pre...  23.3 us
    all_to_all x5, waiting for transfers between devices, spread(): return lax.all_to_all(pieces, LOX, 0, 0, tiled=True)  16.8 us
    pallas_call x1, Pallas kernels, front(): pl.pallas_call(front_kernel, grid=(tokens // STEP,), out_shape=(shape(D,...  13.7 us
    pallas_call x1, Pallas kernels, grad_units(): pl.pallas_call(grad_kernel, grid=(tokens // STEP,), out_shape=(*partial_s...  13.5 us
    pallas_call x1, Pallas kernels, attend_back(): pl.pallas_call(functools.partial(attend_back_kernel, tiles, blocks), out_...  12 us
  transfers between devices with their start and end apart: 53, of which 21 were waited for; matrix products, arithmetic and copies ran while one was open for 22% of the time, Pallas kernels for 17%

profile of v1, /device:TPU:0, one launch (start us, length us, event | category | flops | bytes accessed | tf_op | source)
XLA Modules:
  0.0 413.5 jit_solution(16680262357831707386)
XLA Ops:
  4.6 7.3 %all-to-all-start = ((bf16[8,400,128]{2,1,0:T(8,128)(2,1)}), bf16[8,400,128]{2,1,0:T(8,128)(2,1)S(1)}, u32[]{:S(2)}, u32[]{:S(2)}) async-start(bf16[8,400,128]{2,1,0:T(8,128)(2,1)} %pack.1), calls=%async_computation | async-start | bytes 1638400 | tf_op jit(solution)/shard_map/all_to_all | solution.py:38
  16.0 16.8 %all-to-all-done.own = bf16[8,400,128]{2,1,0:T(8,128)(2,1)S(1)} async-done(((bf16[8,400,128]{2,1,0:T(8,128)(2,1)}), bf16[8,400,128]{2,1,0:T(8,128)(2,1)S(1)}, u32[]{:S(2)}, u32[]{:S(2)}) %all-to-all-start) | async-done | bytes 819232 | tf_op jit(solution)/shard_map/all_to_all | solution.py:38
  32.8 4.2 %all-to-all-start.1 = ((bf16[8,1,256,256]{3,2,1,0:T(8,128)(2,1)}), bf16[8,1,256,256]{3,2,1,0:T(8,128)(2,1)}, u32[]{:S(2)}, u32[]{:S(2)}) async-start(bf16[8,1,256,256]{3,2,1,0:T(8,128)(2,1)} %copy.110), calls=%async_computation.1 | async-start | bytes 2097152 | tf_op jit(solution)/shard_map/all_to_all | solution.py:38
  43.0 2.9 collective-permute-start.1
  46.3 34.6 %collective-permute-done.1 = bf16[2,64,1024]{2,1,0:T(8,128)(2,1)S(1)} collective-permute-done((bf16[2,64,1024]{2,1,0:T(8,128)(2,1)S(1)}, bf16[2,64,1024]{2,1,0:T(8,128)(2,1)S(1)}, u32[]{:S(2)}, u32[]{:S(2)}) %collective-permute-start.1) | collective-permute-done | bytes 262176 | tf_op jit(solution)/shard_map/ppermute | solution.py:34
  81.8 3.3 collective-permute-done.23
  85.9 4.3 %all-to-all-start.2 = ((bf16[8,1,320,256]{3,2,1,0:T(8,128)(2,1)}), bf16[8,1,320,256]{3,2,1,0:T(8,128)(2,1)S(1)}, u32[]{:S(2)}, u32[]{:S(2)}) async-start(bf16[8,1,320,256]{3,2,1,0:T(8,128)(2,1)} %maximum_bitcast_fusion), calls=%async_computation.2 | async-start | bytes 2621440 | tf_op jit(solution)/shard_map/all_to_all | solution.py:38
  90.8 6.1 %collective-permute-done.2 = bf16[2,2,64,1024]{3,2,0,1:T(8,128)(2,1)} collective-permute-done((bf16[2,2,64,1024]{3,2,0,1:T(8,128)(2,1)}, bf16[2,2,64,1024]{3,2,0,1:T(8,128)(2,1)}, u32[]{:S(2)}, u32[]{:S(2)}) %collective-permute-start.2) | collective-permute-done | bytes 524320 | tf_op jit(solution)/shard_map/ppermute | solution.py:34
  99.0 4.2 %collective-permute-start.3 = (bf16[4,64,1024]{2,1,0:T(8,128)(2,1)}, bf16[4,64,1024]{2,1,0:T(8,128)(2,1)}, u32[]{:S(2)}, u32[]{:S(2)}) collective-permute-start(bf16[4,64,1024]{2,1,0:T(8,128)(2,1)} %get-tuple-element.103.refs_0_), channel_id=1, source_target_pairs={{0,4},{4,0},{1,5},{5,1},{2,6},{6,2},{3,7},{7,3},{8,12},{12,8},{9,1... | collective-permute-start | bytes 1572872 | tf_op jit(solution)/shard_map/ppermute | solution.py:34
  105.2 16.9 %collective-permute-done.24 = bf16[2,2,64,1024]{3,2,1,0:T(8,128)(2,1)} collective-permute-done((bf16[2,2,64,1024]{3,2,1,0:T(8,128)(2,1)}, bf16[2,2,64,1024]{3,2,1,0:T(8,128)(2,1)}, u32[]{:S(2)}, u32[]{:S(2)}) %collective-permute-start.24) | collective-permute-done | bytes 524320 | tf_op jit(solution)/shard_map/ppermute | solution.py:34
  124.5 3.7 collective-permute-done.7.refs_6_
  131.0 3.2 fusion.4
  134.2 3.0 join.1.refs_10_.refs_13_
  142.1 9.6 %collective-permute-done.8.refs_7_ = bf16[4,64,1024]{2,1,0:T(8,128)(2,1)} collective-permute-done((bf16[4,64,1024]{2,1,0:T(8,128)(2,1)}, bf16[4,64,1024]{2,1,0:T(8,128)(2,1)}, u32[]{:S(2)}, u32[]{:S(2)}) %collective-permute-start.8) | collective-permute-done | bytes 524320 | tf_op jit(solution)/shard_map/ppermute | solution.py:34
  151.8 13.7 %front.1 = (bf16[1024,2048]{1,0:T(8,128)(2,1)}, f32[1024,128]{1,0:T(8,128)}, f32[1024,128]{1,0:T(8,128)}, bf16[1024,128]{1,0:T(8,128)(2,1)}, bf16[1024,128]{1,0:...) custom-call(s32[10]{0:T(128)} %stack.124.place, ...), custom_call_target="tpu_custom_call" | custom-call | flops 3758096384 | bytes 12582912 | tf_op jit(solution)/shard_map/front/pallas_call | solution.py:550
  175.6 9.9 %attend.1 = (bf16[1024,128]{1,0:T(8,128)(2,1)}, f32[1024,128]{1,0:T(8,128)}) custom-call(s32[49]{0:T(128)} %pad_add_fusion.table, bf16[1024,128]{1,0:T(8,128)(2,1)} %get-tuple-element.55.q, bf16[1024,128]{1,0:T(8,128)(2,1)} %get-tuple-element.56.k_own, bf16[1024,128]{1,0:T(8,128)(2,1)} %get-tuple-element.57.v_own, ...), custom_call_target="tpu_custom_call" | custom-call | flops 2684354560 | bytes 2000000 | tf_op jit(solution)/shard_map/attend/pallas_call | solution.py:322
  185.7 7.7 %collective-permute-done.27.refs_3_ = bf16[4,64,1024]{2,1,0:T(8,128)(2,1)} collective-permute-done((bf16[4,64,1024]{2,1,0:T(8,128)(2,1)}, bf16[4,64,1024]{2,1,0:T(8,128)(2,1)}, u32[]{:S(2)}, u32[]{:S(2)}) %collective-permute-start.27) | collective-permute-done | bytes 524320 | tf_op jit(solution)/shard_map/ppermute | solution.py:34
  196.1 9.9 %back.1 = (bf16[1024,2048]{1,0:T(8,128)(2,1)}, bf16[1024,512]{1,0:T(8,128)(2,1)}, bf16[1024,128]{1,0:T(8,128)(2,1)}, f32[1,512]{1,0:T(1,128)}) custom-call(s32[10]{0:T(128)} %stack.124.place, bf16[4,64,1024]{2,1,0:T(8,128)(2,1)} %get-tuple-element.101.refs_0_, bf16[4,64,1024]{2,1,0:T(8,128)(2,1)} %collective-permute-done.25.refs_1_, ...), custom_call_target="tpu_custom_call" | custom-call | flops 2684354560 | bytes 14000000 | tf_op jit(solution)/shard_map/back/pallas_call | solution.py:725
  206.1 4.6 %convolution_convert_fusion.1 = bf16[256,2048]{1,0:T(8,128)(2,1)} fusion(bf16[1024,2048]{1,0:T(8,128)(2,1)} %get-tuple-element.70, bf16[1024,512]{1,0:T(8,128)(2,1)S(1)} %copy-done.66), kind=kOutput, calls=%fused_computation.3 | convolution fusion | flops 1074266112 | bytes 5767168 | tf_op jit(solution)/shard_map/dot_general | solution.py:73
  213.4 8.6 %mix.1 = (bf16[8,64,1024]{2,1,0:T(8,128)(2,1)}, bf16[8,64,1024]{2,1,0:T(8,128)(2,1)}, bf16[4,2,64,1024]{3,2,1,0:T(8,128)(2,1)}, bf16[4,2,64,1024]{3,2,1,0:T(8,128)(2,1)}) custom-call(s32[10]{0:T(128)} %stack.124.place, bf16[1024,128]{1,0:T(8,128)(2,1)} %get-tuple-element.59.attended.att, bf16[1024,512]{1,0:T(8,128)(2,1)} %get-tuple-element.60.active, ...), custom_call_target="tpu_custom_call" | custom-call | flops 2684354560 | bytes 8000000 | tf_op jit(solution)/shard_map/mix/pallas_call | solution.py:661
  223.5 3.2 fusion.1
  231.4 12.0 %attend_back.1 = (f32[1024,128]{1,0:T(8,128)}, f32[1024,128]{1,0:T(8,128)}, f32[1024,128]{1,0:T(8,128)}, bf16[2,1024,128]{2,1,0:T(8,128)(2,1)}) custom-call(s32[49]{0:T(128)} %pad_add_fusion.table, bf16[1024,128]{1,0:T(8,128)(2,1)} %get-tuple-element.55.q, bf16[1024,128]{1,0:T(8,128)(2,1)} %get-tuple-element.56.k_own, ...), custom_call_target="tpu_custom_call" | custom-call | flops 6710886400 | bytes 6000000 | tf_op jit(solution)/shard_map/attend_back/pallas_call | solution.py:454
  243.4 4.1 all-to-all-start.4
  258.5 4.2 %unturn.1 = (bf16[1024,384]{1,0:T(8,128)(2,1)}, bf16[1024,192]{1,0:T(8,128)(2,1)}, bf16[1024,192]{1,0:T(8,128)(2,1)}, f32[1,384]{1,0:T(1,128)}) custom-call(f32[1024,128]{1,0:T(8,128)} %get-tuple-element.73.dq, f32[1024,128]{1,0:T(8,128)} %get-tuple-element.74.dk, f32[1024,128]{1,0:T(8,128)} %get-tuple-element.75.dv, ...), custom_call_target="tpu_custom_call" | custom-call | bytes 6000000 | tf_op jit(solution)/shard_map/unturn/pallas_call | solution.py:767
  262.7 13.5 %grad.1 = (bf16[8,64,1024]{2,1,0:T(8,128)(2,1)}, bf16[8,64,1024]{2,1,0:T(8,128)(2,1)}, bf16[4,2,64,1024]{3,2,1,0:T(8,128)(2,1)}, bf16[4,2,64,1024]{3,2,1,0:T(8,1...) custom-call(s32[10]{0:T(128)} %stack.124.place, ...), custom_call_target="tpu_custom_call" | custom-call | flops 3758096384 | bytes 16000000 | tf_op jit(solution)/shard_map/grad/pallas_call | solution.py:836
  276.3 4.8 %convolution_convert_fusion = bf16[2048,256]{1,0:T(8,128)(2,1)} fusion(bf16[1024,2048]{1,0:T(8,128)(2,1)} %get-tuple-element.92, bf16[1024,512]{1,0:T(8,128)(2,1)} %get-tuple-element.78.refs_12_), kind=kOutput, calls=%fused_computation.2 | convolution fusion | flops 1074266112 | bytes 5767168 | tf_op jit(solution)/shard_map/dot_general | solution.py:73
  315.2 4.5 %collective-permute-done.34 = bf16[8,64,1024]{2,1,0:T(8,128)(2,1)} collective-permute-done((bf16[8,64,1024]{2,1,0:T(8,128)(2,1)}, bf16[8,64,1024]{2,1,0:T(8,128)(2,1)}, u32[]{:S(2)}, u32[]{:S(2)}) %collective-permute-start.34) | collective-permute-done | bytes 1048608 | tf_op jit(solution)/shard_map/ppermute | solution.py:34
  335.0 4.6 %pack_grad.1 = bf16[8,448,256]{2,1,0:T(8,128)(2,1)} custom-call(f32[2048,256]{1,0:T(8,128)} %fusion.21.fc1_own, bf16[2048,256]{1,0:T(8,128)(2,1)} %collective-permute-done.46.fc1_other, f32[2048,192]{1,0:T(8,128)} %fusion.58.own, bf16[2048,192]{1,0:T(8,128)(2,1)} %copy.122.other), custom_call_target="tpu_custom_call" | custom-call | bytes 9000000 | tf_op jit(solution)/shard_map/pack_grad/pallas_call | solution.py:182
  341.7 3.6 all-to-all-start.3
  357.9 28.7 %collective-permute-done.38 = bf16[2,2,64,1024]{3,2,0,1:T(8,128)(2,1)} collective-permute-done((bf16[2,2,64,1024]{3,2,0,1:T(8,128)(2,1)}, bf16[2,2,64,1024]{3,2,0,1:T(8,128)(2,1)}, u32[]{:S(2)}, u32[]{:S(2)}) %collective-permute-start.38) | collective-permute-done | bytes 524320 | tf_op jit(solution)/shard_map/ppermute | solution.py:34
  392.5 7.1 %collective-permute-done.39 = bf16[2,64,1024]{2,1,0:T(8,128)(2,1)S(1)} collective-permute-done((bf16[2,64,1024]{2,1,0:T(8,128)(2,1)S(1)}, bf16[2,64,1024]{2,1,0:T(8,128)(2,1)S(1)}, u32[]{:S(2)}, u32[]{:S(2)}) %collective-permute-start.39) | collective-permute-done | bytes 262176 | tf_op jit(solution)/shard_map/ppermute | solution.py:34
  409.0 3.7 home.1
  (385 shorter events, 142.8 us)
Async XLA Ops:
  4.6 28.2 %all-to-all-start = ((bf16[8,400,128]{2,1,0:T(8,128)(2,1)}), bf16[8,400,128]{2,1,0:T(8,128)(2,1)S(1)}, u32[]{:S(2)}, u32[]{:S(2)}) async-start(bf16[8,400,128]{2,1,0:T(8,128)(2,1)} %pack.1), calls=%async_computation | async-start | bytes 1638400 | tf_op jit(solution)/shard_map/all_to_all | solution.py:38
  12.6 30.3 %collective-permute-start = (bf16[128,512]{1,0:T(8,128)(2,1)}, bf16[128,512]{1,0:T(8,128)(2,1)S(1)}, u32[]{:S(2)}, u32[]{:S(2)}) collective-permute-start(bf16[128,512]{1,0:T(8,128)(2,1)} %bitcast.12), channel_id=1, source_target_pairs={{0,1},{1,0},{2,3},{3,2},{4,5},{5,4},{6,7},{7,6},{8,9},{9,8},{10,11... | collective-permute-start | bytes 393224 | tf_op jit(solution)/shard_map/ppermute | solution.py:34
  13.6 25.5 %collective-permute-start.9 = (f32[1472]{0:T(1024)S(1)}, f32[1472]{0:T(1024)S(1)}, u32[]{:S(2)}, u32[]{:S(2)}) collective-permute-start(f32[1472]{0:T(1024)S(1)} %concatenate.174), channel_id=1, source_target_pairs={{0,1},{1,0},{2,3},{3,2},{4,5},{5,4},{6,7},{7,6},{8,9},{9,8},{10,11... | collective-permute-start | bytes 17672 | tf_op jit(solution)/shard_map/ppermute | solution.py:34
  32.8 53.1 %all-to-all-start.1 = ((bf16[8,1,256,256]{3,2,1,0:T(8,128)(2,1)}), bf16[8,1,256,256]{3,2,1,0:T(8,128)(2,1)}, u32[]{:S(2)}, u32[]{:S(2)}) async-start(bf16[8,1,256,256]{3,2,1,0:T(8,128)(2,1)} %copy.110), calls=%async_computation.1 | async-start | bytes 2097152 | tf_op jit(solution)/shard_map/all_to_all | solution.py:38
  43.0 37.9 %collective-permute-start.1 = (bf16[2,64,1024]{2,1,0:T(8,128)(2,1)S(1)}, bf16[2,64,1024]{2,1,0:T(8,128)(2,1)S(1)}, u32[]{:S(2)}, u32[]{:S(2)}) collective-permute-start(bf16[2,64,1024]{2,1,0:T(8,128)(2,1)S(1)} %maximum_select_fusion.3), channel_id=1, source_target_pairs={{0,16},{16,0},{1,17},{17,1},{2,18},{18,2},{3,19},{19,3},{4,20},{20... | collective-permute-start | bytes 786440 | tf_op jit(solution)/shard_map/ppermute | solution.py:34
  45.9 39.1 %collective-permute-start.23 = (bf16[2,64,1024]{2,1,0:T(8,128)(2,1)S(1)}, bf16[2,64,1024]{2,1,0:T(8,128)(2,1)S(1)}, u32[]{:S(2)}, u32[]{:S(2)}) collective-permute-start(bf16[2,64,1024]{2,1,0:T(8,128)(2,1)S(1)} %maximum_select_fusion.5), channel_id=1, source_target_pairs={{0,16},{16,0},{1,17},{17,1},{2,18},{18,2},{3,19},{19,3},{4,20},{20... | collective-permute-start | bytes 786440 | tf_op jit(solution)/shard_map/ppermute | solution.py:34
  85.9 36.3 %collective-permute-start.24 = (bf16[2,2,64,1024]{3,2,1,0:T(8,128)(2,1)}, bf16[2,2,64,1024]{3,2,1,0:T(8,128)(2,1)}, u32[]{:S(2)}, u32[]{:S(2)}) collective-permute-start(bf16[2,2,64,1024]{3,2,1,0:T(8,128)(2,1)} %pad_maximum_fusion.6), channel_id=1, source_target_pairs={{0,8},{8,0},{1,9},{9,1},{2,10},{10,2},{3,11},{11,3},{4,12},{12,4},... | collective-permute-start | bytes 1572872 | tf_op jit(solution)/shard_map/ppermute | solution.py:34
  85.9 56.1 %all-to-all-start.2 = ((bf16[8,1,320,256]{3,2,1,0:T(8,128)(2,1)}), bf16[8,1,320,256]{3,2,1,0:T(8,128)(2,1)S(1)}, u32[]{:S(2)}, u32[]{:S(2)}) async-start(bf16[8,1,320,256]{3,2,1,0:T(8,128)(2,1)} %maximum_bitcast_fusion), calls=%async_computation.2 | async-start | bytes 2621440 | tf_op jit(solution)/shard_map/all_to_all | solution.py:38
  99.0 25.4 %collective-permute-start.3 = (bf16[4,64,1024]{2,1,0:T(8,128)(2,1)}, bf16[4,64,1024]{2,1,0:T(8,128)(2,1)}, u32[]{:S(2)}, u32[]{:S(2)}) collective-permute-start(bf16[4,64,1024]{2,1,0:T(8,128)(2,1)} %get-tuple-element.103.refs_0_), channel_id=1, source_target_pairs={{0,4},{4,0},{1,5},{5,1},{2,6},{6,2},{3,7},{7,3},{8,12},{12,8},{9,1... | collective-permute-start | bytes 1572872 | tf_op jit(solution)/shard_map/ppermute | solution.py:34
  103.2 34.0 %collective-permute-start.4 = (bf16[4,64,1024]{2,1,0:T(8,128)(2,1)}, bf16[4,64,1024]{2,1,0:T(8,128)(2,1)}, u32[]{:S(2)}, u32[]{:S(2)}) collective-permute-start(bf16[4,64,1024]{2,1,0:T(8,128)(2,1)} %get-tuple-element.103.refs_0_), channel_id=1, source_target_pairs={{0,2},{2,0},{1,3},{3,1},{4,6},{6,4},{5,7},{7,5},{8,10},{10,8},{9,1... | collective-permute-start | bytes 1572872 | tf_op jit(solution)/shard_map/ppermute | solution.py:34
  104.7 23.5 %collective-permute-start.7 = (bf16[4,64,1024]{2,1,0:T(8,128)(2,1)S(1)}, bf16[4,64,1024]{2,1,0:T(8,128)(2,1)}, u32[]{:S(2)}, u32[]{:S(2)}) collective-permute-start(bf16[4,64,1024]{2,1,0:T(8,128)(2,1)S(1)} %get-tuple-element.102.refs_4_), channel_id=1, source_target_pairs={{0,2},{2,0},{1,3},{3,1},{4,6},{6,4},{5,7},{7,5},{8,10},{10,8},{9,1... | collective-permute-start | bytes 1572872 | tf_op jit(solution)/shard_map/ppermute | solution.py:34
  105.2 24.5 %collective-permute-start.11 = (bf16[8,400,128]{2,1,0:T(8,128)(2,1)S(1)}, bf16[8,400,128]{2,1,0:T(8,128)(2,1)S(1)}, u32[]{:S(2)}, u32[]{:S(2)}) collective-permute-start(bf16[8,400,128]{2,1,0:T(8,128)(2,1)S(1)} %all-to-all-done.own), channel_id=1, source_target_pairs={{0,1},{1,0},{2,3},{3,2},{4,5},{5,4},{6,7},{7,6},{8,9},{9,8},{10,11... | collective-permute-start | bytes 2457608 | tf_op jit(solution)/shard_map/ppermute | solution.py:34
  124.4 27.4 %collective-permute-start.12 = (bf16[2048,256]{1,0:T(8,128)(2,1)}, bf16[2048,256]{1,0:T(8,128)(2,1)}, u32[]{:S(2)}, u32[]{:S(2)}) collective-permute-start(bf16[2048,256]{1,0:T(8,128)(2,1)} %bitcast.33.refs_15_.refs_14_), channel_id=1, source_target_pairs={{0,1},{1,0},{2,3},{3,2},{4,5},{5,4},{6,7},{7,6},{8,9},{9,8},{10,11... | collective-permute-start | bytes 3145736 | tf_op jit(solution)/shard_map/ppermute | solution.py:34
  130.7 21.1 %collective-permute-start.8 = (bf16[4,64,1024]{2,1,0:T(8,128)(2,1)}, bf16[4,64,1024]{2,1,0:T(8,128)(2,1)}, u32[]{:S(2)}, u32[]{:S(2)}) collective-permute-start(bf16[4,64,1024]{2,1,0:T(8,128)(2,1)} %collective-permute-done.7.refs_6_), channel_id=1, source_target_pairs={{0,4},{4,0},{1,5},{5,1},{2,6},{6,2},{3,7},{7,3},{8,12},{12,8},{9,1... | collective-permute-start | bytes 1572872 | tf_op jit(solution)/shard_map/ppermute | solution.py:34
  137.2 33.6 %collective-permute-start.25 = (bf16[4,64,1024]{2,1,0:T(8,128)(2,1)S(1)}, bf16[4,64,1024]{2,1,0:T(8,128)(2,1)}, u32[]{:S(2)}, u32[]{:S(2)}) collective-permute-start(bf16[4,64,1024]{2,1,0:T(8,128)(2,1)S(1)} %copy-done.39), channel_id=1, source_target_pairs={{0,4},{4,0},{1,5},{5,1},{2,6},{6,2},{3,7},{7,3},{8,12},{12,8},{9,1... | collective-permute-start | bytes 1572872 | tf_op jit(solution)/shard_map/ppermute | solution.py:34
  140.5 30.3 %collective-permute-start.29 = (bf16[4,64,1024]{2,1,0:T(8,128)(2,1)S(1)}, bf16[4,64,1024]{2,1,0:T(8,128)(2,1)}, u32[]{:S(2)}, u32[]{:S(2)}) collective-permute-start(bf16[4,64,1024]{2,1,0:T(8,128)(2,1)S(1)} %copy-done.38), channel_id=1, source_target_pairs={{0,2},{2,0},{1,3},{3,1},{4,6},{6,4},{5,7},{7,5},{8,10},{10,8},{9,1... | collective-permute-start | bytes 1572872 | tf_op jit(solution)/shard_map/ppermute | solution.py:34
  142.0 54.1 %collective-permute-start.14 = (bf16[8,320,256]{2,1,0:T(8,128)(2,1)S(1)}, bf16[8,320,256]{2,1,0:T(8,128)(2,1)}, u32[]{:S(2)}, u32[]{:S(2)}) collective-permute-start(bf16[8,320,256]{2,1,0:T(8,128)(2,1)S(1)} %bitcast.236), channel_id=1, source_target_pairs={{0,1},{1,0},{2,3},{3,2},{4,5},{5,4},{6,7},{7,6},{8,9},{9,8},{10,11... | collective-permute-start | bytes 3932168 | tf_op jit(solution)/shard_map/ppermute | solution.py:34
  170.8 22.6 %collective-permute-start.27 = (bf16[4,64,1024]{2,1,0:T(8,128)(2,1)}, bf16[4,64,1024]{2,1,0:T(8,128)(2,1)}, u32[]{:S(2)}, u32[]{:S(2)}) collective-permute-start(bf16[4,64,1024]{2,1,0:T(8,128)(2,1)} %collective-permute-done.25.refs_1_), channel_id=1, source_target_pairs={{0,2},{2,0},{1,3},{3,1},{4,6},{6,4},{5,7},{7,5},{8,10},{10,8},{9,1... | collective-permute-start | bytes 1572872 | tf_op jit(solution)/shard_map/ppermute | solution.py:34
  171.4 24.8 %collective-permute-start.30 = (bf16[4,64,1024]{2,1,0:T(8,128)(2,1)}, bf16[4,64,1024]{2,1,0:T(8,128)(2,1)}, u32[]{:S(2)}, u32[]{:S(2)}) collective-permute-start(bf16[4,64,1024]{2,1,0:T(8,128)(2,1)} %collective-permute-done.29.refs_6_), channel_id=1, source_target_pairs={{0,4},{4,0},{1,5},{5,1},{2,6},{6,2},{3,7},{7,3},{8,12},{12,8},{9,1... | collective-permute-start | bytes 1572872 | tf_op jit(solution)/shard_map/ppermute | solution.py:34
  222.0 25.5 %collective-permute-start.15 = (bf16[8,64,1024]{2,1,0:T(8,128)(2,1)}, bf16[8,64,1024]{2,1,0:T(8,128)(2,1)S(1)}, u32[]{:S(2)}, u32[]{:S(2)}) collective-permute-start(bf16[8,64,1024]{2,1,0:T(8,128)(2,1)} %get-tuple-element.62), channel_id=1, source_target_pairs={{0,2},{2,0},{1,3},{3,1},{4,6},{6,4},{5,7},{7,5},{8,10},{10,8},{9,1... | collective-permute-start | bytes 3145736 | tf_op jit(solution)/shard_map/ppermute | solution.py:34
  222.6 30.9 %collective-permute-start.17 = (bf16[4,2,64,1024]{3,2,1,0:T(8,128)(2,1)}, bf16[4,2,64,1024]{3,2,1,0:T(8,128)(2,1)S(1)}, u32[]{:S(2)}, u32[]{:S(2)}) collective-permute-start(bf16[4,2,64,1024]{3,2,1,0:T(8,128)(2,1)} %get-tuple-element.64), channel_id=1, source_target_pairs={{0,4},{4,0},{1,5},{5,1},{2,6},{6,2},{3,7},{7,3},{8,12},{12,8},{9,1... | collective-permute-start | bytes 3145736 | tf_op jit(solution)/shard_map/ppermute | solution.py:34
  243.4 98.2 %all-to-all-start.4 = ((bf16[8,1,320,256]{3,2,1,0:T(8,128)(2,1)}), bf16[8,1,320,256]{3,2,1,0:T(8,128)(2,1)S(1)}, u32[]{:S(2)}, u32[]{:S(2)}) async-start(bf16[8,1,320,256]{3,2,1,0:T(8,128)(2,1)} %pad_maximum_fusion), calls=%async_computation.4 | async-start | bytes 2621440 | tf_op jit(solution)/shard_map/all_to_all | solution.py:38
  251.5 43.2 %collective-permute-start.16 = (bf16[4,64,1024]{2,1,0:T(8,128)(2,1)}, bf16[4,64,1024]{2,1,0:T(8,128)(2,1)}, u32[]{:S(2)}, u32[]{:S(2)}) collective-permute-start(bf16[4,64,1024]{2,1,0:T(8,128)(2,1)} %slice.365), channel_id=1, source_target_pairs={{0,4},{4,0},{1,5},{5,1},{2,6},{6,2},{3,7},{7,3},{8,12},{12,8},{9,1... | collective-permute-start | bytes 1572872 | tf_op jit(solution)/shard_map/ppermute | solution.py:34
  257.0 43.6 %collective-permute-start.18 = (bf16[4,64,1024]{2,1,0:T(8,128)(2,1)}, bf16[4,64,1024]{2,1,0:T(8,128)(2,1)S(1)}, u32[]{:S(2)}, u32[]{:S(2)}) collective-permute-start(bf16[4,64,1024]{2,1,0:T(8,128)(2,1)} %slice_bitcast_fusion.4), channel_id=1, source_target_pairs={{0,2},{2,0},{1,3},{3,1},{4,6},{6,4},{5,7},{7,5},{8,10},{10,8},{9,1... | collective-permute-start | bytes 1572872 | tf_op jit(solution)/shard_map/ppermute | solution.py:34
  285.6 47.1 %collective-permute-start.47 = (bf16[2048,192]{0,1:T(8,128)(2,1)}, bf16[2048,192]{0,1:T(8,128)(2,1)}, u32[]{:S(2)}, u32[]{:S(2)}) collective-permute-start(bf16[2048,192]{0,1:T(8,128)(2,1)} %convolution_convert_fusion.2), channel_id=1, source_target_pairs={{0,1},{1,0},{2,3},{3,2},{4,5},{5,4},{6,7},{7,6},{8,9},{9,8},{10,11... | collective-permute-start | bytes 2359304 | tf_op jit(solution)/shard_map/ppermute | solution.py:34
  288.4 46.6 %collective-permute-start.46 = (bf16[2048,256]{1,0:T(8,128)(2,1)}, bf16[2048,256]{1,0:T(8,128)(2,1)}, u32[]{:S(2)}, u32[]{:S(2)}) collective-permute-start(bf16[2048,256]{1,0:T(8,128)(2,1)} %convolution_convert_fusion), channel_id=1, source_target_pairs={{0,1},{1,0},{2,3},{3,2},{4,5},{5,4},{6,7},{7,6},{8,9},{9,8},{10,11... | collective-permute-start | bytes 3145736 | tf_op jit(solution)/shard_map/ppermute | solution.py:34
  294.2 25.5 %collective-permute-start.34 = (bf16[8,64,1024]{2,1,0:T(8,128)(2,1)}, bf16[8,64,1024]{2,1,0:T(8,128)(2,1)}, u32[]{:S(2)}, u32[]{:S(2)}) collective-permute-start(bf16[8,64,1024]{2,1,0:T(8,128)(2,1)} %get-tuple-element.84), channel_id=1, source_target_pairs={{0,2},{2,0},{1,3},{3,1},{4,6},{6,4},{5,7},{7,5},{8,10},{10,8},{9,1... | collective-permute-start | bytes 3145736 | tf_op jit(solution)/shard_map/ppermute | solution.py:34
  299.1 24.5 %collective-permute-start.36 = (bf16[4,2,64,1024]{3,2,1,0:T(8,128)(2,1)}, bf16[4,2,64,1024]{3,2,1,0:T(8,128)(2,1)}, u32[]{:S(2)}, u32[]{:S(2)}) collective-permute-start(bf16[4,2,64,1024]{3,2,1,0:T(8,128)(2,1)} %get-tuple-element.86), channel_id=1, source_target_pairs={{0,4},{4,0},{1,5},{5,1},{2,6},{6,2},{3,7},{7,3},{8,12},{12,8},{9,1... | collective-permute-start | bytes 3145736 | tf_op jit(solution)/shard_map/ppermute | solution.py:34
  330.4 21.4 %collective-permute-start.20 = (bf16[2,64,1024]{2,1,0:T(8,128)(2,1)}, bf16[2,64,1024]{2,1,0:T(8,128)(2,1)}, u32[]{:S(2)}, u32[]{:S(2)}) collective-permute-start(bf16[2,64,1024]{2,1,0:T(8,128)(2,1)} %slice_bitcast_fusion.10), channel_id=1, source_target_pairs={{0,16},{16,0},{1,17},{17,1},{2,18},{18,2},{3,19},{19,3},{4,20},{20... | collective-permute-start | bytes 786440 | tf_op jit(solution)/shard_map/ppermute | solution.py:34
  341.7 66.1 %all-to-all-start.3 = ((bf16[8,448,256]{2,1,0:T(8,128)(2,1)}), bf16[8,448,256]{2,1,0:T(8,128)(2,1)S(1)}, u32[]{:S(2)}, u32[]{:S(2)}) async-start(bf16[8,448,256]{2,1,0:T(8,128)(2,1)} %pack_grad.1), calls=%async_computation.3 | async-start | bytes 3670016 | tf_op jit(solution)/shard_map/all_to_all | solution.py:38
  349.3 37.2 %collective-permute-start.38 = (bf16[2,2,64,1024]{3,2,0,1:T(8,128)(2,1)}, bf16[2,2,64,1024]{3,2,0,1:T(8,128)(2,1)}, u32[]{:S(2)}, u32[]{:S(2)}) collective-permute-start(bf16[2,2,64,1024]{3,2,0,1:T(8,128)(2,1)} %pad_maximum_fusion.3), channel_id=1, source_target_pairs={{0,8},{8,0},{1,9},{9,1},{2,10},{10,2},{3,11},{11,3},{4,12},{12,4},... | collective-permute-start | bytes 1572872 | tf_op jit(solution)/shard_map/ppermute | solution.py:34
  357.7 32.8 %collective-permute-start.21 = (f32[128,512]{1,0:T(8,128)S(1)}, f32[128,512]{1,0:T(8,128)S(1)}, u32[]{:S(2)}, u32[]{:S(2)}) collective-permute-start(f32[128,512]{1,0:T(8,128)S(1)} %bitcast.261), channel_id=1, source_target_pairs={{0,1},{1,0},{2,3},{3,2},{4,5},{5,4},{6,7},{7,6},{8,9},{9,8},{10,11... | collective-permute-start | bytes 786440 | tf_op jit(solution)/shard_map/ppermute | solution.py:34
  (89 other events, 1092.3 us)

commit v2 on v1

--- a/solution.py
+++ b/solution.py
@@ -115,49 +115,65 @@
     ]
 
 
-def pack_kernel(weight, ids, out):
+def pack_kernel(fc1, weight, ids, out):
     for c in range(LO):
-        out[c, 3 * BLK :] = ids[...]
         columns = slice(c * HD, (c + 1) * HD)
-        for j in range(3):
-            out[c, j * BLK : (j + 1) * BLK] = jnp.concatenate(
-                [weight[j, :BLK, columns], weight[j, BLK:, columns]], axis=1
-            )
-
-
-def pack_heads(weight, ids):
+        out[c, : 2 * BLK] = fc1[:, c * 256 : (c + 1) * 256]
+        tiles = [
+            jnp.concatenate([weight[j, :BLK, columns], weight[j, BLK:, columns]], axis=1)
+            for j in range(3)
+        ]
+        out[c, 2 * BLK : 3 * BLK] = jnp.concatenate(tiles[:2], axis=1)
+        out[c, 3 * BLK : 3 * BLK + HALF] = jnp.concatenate(
+            [tiles[2][:HALF], tiles[2][HALF:]], axis=1
+        )
+        out[c, 3 * BLK + HALF :] = ids[...]
+
+
+def pack_first(fc1, weight, ids):
     return pl.pallas_call(
         pack_kernel,
-        out_shape=jax.ShapeDtypeStruct((LO, 3 * BLK + IDS, BLK), BF),
-        in_specs=full_spec(2),
+        out_shape=jax.ShapeDtypeStruct((LO, 3 * BLK + HALF + IDS, 256), BF),
+        in_specs=full_spec(3),
         out_specs=full_spec(1)[0],
-        cost_estimate=cost(0, 1600000),
+        cost_estimate=cost(0, 3800000),
         name="pack",
-    )(weight, ids)
-
-
-def join_kernel(own, other, out):
+    )(fc1, weight, ids)
+
+
+def head_tile(half, c, j):
+    if j < 2:
+        return half[c, 2 * BLK : 3 * BLK, j * BLK : (j + 1) * BLK]
+    rows = slice(3 * BLK, 3 * BLK + HALF)
+    return jnp.concatenate([half[c, rows, :BLK], half[c, rows, BLK:]], axis=0)
+
+
+def join_kernel(own, other, fc1_own, fc1_other, qkv):
     for c in range(LO):
-        for u in range(2):
-            columns = slice(u * HD, (u + 1) * HD)
-            rows = pl.ds(c * 2 * BLK + u * BLK, BLK)
-            for j in range(3):
-                out[rows, j * BLK : (j + 1) * BLK] = jnp.concatenate(
-                    [
-                        half[c, j * BLK : (j + 1) * BLK, columns]
-                        for half in (own, other)
-                    ],
-                    axis=1,
+        rows = pl.ds(c * 2 * BLK, 2 * BLK)
+        fc1_own[rows, :] = own[c, : 2 * BLK]
+        fc1_other[rows, :] = other[c, : 2 * BLK]
+        for j in range(3):
+            tiles = [head_tile(half, c, j) for half in (own, other)]
+            for u in range(2):
+                columns = slice(u * HD, (u + 1) * HD)
+                rows = pl.ds(c * 2 * BLK + u * BLK, BLK)
+                qkv[rows, j * BLK : (j + 1) * BLK] = jnp.concatenate(
+                    [tile[:, columns] for tile in tiles], axis=1
                 )
 
 
-def join_heads(own, other):
+def join_first(own, other):
     return pl.pallas_call(
         join_kernel,
-        out_shape=jax.ShapeDtypeStruct((D, 3 * BLK), BF),
+        out_shape=(
+            jax.ShapeDtypeStruct((D, 256), BF),
+            jax.ShapeDtypeStruct((D, 256), BF),
+            jax.ShapeDtypeStruct((D, 3 * BLK), BF),
+        ),
         in_specs=full_spec(2),
-        out_specs=full_spec(1)[0],
-        cost_estimate=cost(0, 3200000),
+        out_specs=tuple(full_spec(3)),
+        cost_estimate=cost(0, 7400000),
         name="join",
     )(own, other)
 
@@ -634,30 +650,25 @@
     )
 
 
-def out_rows(c, down_own, down_other):
-    hidden = down_own.shape[1] - HD
-    return jnp.concatenate([down_own[c, hidden:], down_other[c, hidden:]], axis=0)
-
-
-def mix_kernel(place, attended, active, down_own, down_other, *partial):
-    hidden = down_own.shape[1] - HD
+def mix_kernel(place, attended, active, out2, fc2_own, fc2_other, *partial):
+    hidden = fc2_own.shape[1]
     for index, side in enumerate((place[0], 1 - place[0])):
         parts = []
         for quarter in range(4):
             c = 4 * side + quarter
             parts.append(
                 (
-                    dot(active[:, :hidden], down_own[c, :hidden], 1, 0)
-                    + dot(active[:, hidden:], down_other[c, :hidden], 1, 0)
-                    + dot(attended[...], out_rows(c, down_own, down_other), 1, 0)
+                    dot(active[:, :hidden], fc2_own[c], 1, 0)
+                    + dot(active[:, hidden:], fc2_other[c], 1, 0)
+                    + dot(attended[...], out2[c], 1, 0)
                 ).astype(BF)
             )
         store_pieces(pl.program_id(0), index, jnp.concatenate(parts, axis=1), *partial)
 
 
-def mix(place, attended, active, down_own, down_other):
+def mix(place, attended, active, out2, fc2_own, fc2_other):
     tokens = LO * BLK
-    hidden = down_own.shape[1] - HD
+    hidden = fc2_own.shape[1]
     return pl.pallas_call(
         mix_kernel,
         grid=(tokens // STEP,),
@@ -666,13 +677,14 @@
             scalar_spec(),
             rows_spec(BLK),
             rows_spec(2 * hidden),
-            fixed_spec(LO, hidden + HD, 256),
-            fixed_spec(LO, hidden + HD, 256),
+            fixed_spec(LO, BLK, 256),
+            fixed_spec(LO, hidden, 256),
+            fixed_spec(LO, hidden, 256),
         ],
         out_specs=partial_specs(),
         cost_estimate=cost(2 * tokens * D * (128 + 2 * hidden), 8000000),
         name="mix",
-    )(place, attended, active, down_own, down_other)
+    )(place, attended, active, out2, fc2_own, fc2_other)
 
 
 def back_kernel(place, *refs):
@@ -683,8 +695,9 @@
     place,
     pieces,
     pre,
-    down_own,
-    down_other,
+    out2,
+    fc2_own,
+    fc2_other,
     cot,
     grad_pre,
     grad_attended,
@@ -698,30 +711,30 @@
     for part, side in zip(parts, sides_of(place)):
         cot[:, side] = part
     rows = cot[...]
-    hidden = down_own.shape[1] - HD
+    hidden = fc2_own.shape[1]
 
     def through(weight):
         total = 0.0
         for c in range(LO):
-            total = total + dot(rows[:, c * 256 : (c + 1) * 256], weight(c), 1, 1)
+            total = total + dot(rows[:, c * 256 : (c + 1) * 256], weight[c], 1, 1)
         return total
 
-    grad_attended[...] = through(lambda c: out_rows(c, down_own, down_other)).astype(BF)
-    for part, weight in enumerate((down_own, down_other)):
+    grad_attended[...] = through(out2).astype(BF)
+    for part, weight in enumerate((fc2_own, fc2_other)):
         columns = slice(part * hidden, (part + 1) * hidden)
         value = pre[:, columns]
         inner = jnp.tanh(inner_coef * (value + cubic_coef * value * value * value))
         slope = 0.5 * (1.0 + inner) + 0.5 * value * (1.0 - inner * inner) * inner_coef * (
             1.0 + 3.0 * cubic_coef * value * value
         )
-        grad = through(lambda c: weight[c, :hidden]) * slope
+        grad = through(weight) * slope
         bias_sum[:, columns] += jnp.sum(grad, axis=0, keepdims=True)
         grad_pre[:, columns] = grad.astype(BF)
 
 
-def back(place, pieces, pre, down_own, down_other):
+def back(place, pieces, pre, out2, fc2_own, fc2_other):
     tokens = LO * BLK
-    hidden = down_own.shape[1] - HD
+    hidden = fc2_own.shape[1]
     return pl.pallas_call(
         back_kernel,
         grid=(tokens // STEP,),
@@ -735,8 +748,9 @@
             scalar_spec(),
             *piece_specs(),
             rows_spec(2 * hidden),
-            fixed_spec(LO, hidden + HD, 256),
-            fixed_spec(LO, hidden + HD, 256),
+            fixed_spec(LO, BLK, 256),
+            fixed_spec(LO, hidden, 256),
+            fixed_spec(LO, hidden, 256),
         ],
         out_specs=(
             rows_spec(D),
@@ -746,7 +760,7 @@
         ),
         cost_estimate=cost(2 * tokens * D * (128 + 2 * hidden), 14000000),
         name="back",
-    )(place, *pieces, pre, down_own, down_other)
+    )(place, *pieces, pre, out2, fc2_own, fc2_other)
 
 
 def unturn_kernel(dq, dk, dv, got, cosine, sine_a, sine_b, joint, own, other, bias):
@@ -918,9 +932,6 @@
     def ordered(got, shape):
         return got if n_hi == 1 else jnp.moveaxis(got, 1, 0).reshape(shape)
 
-    fc1_own = spread(over_hi(w_fc1).reshape(n_hi, depth, LO, hidden).transpose(2, 0, 1, 3))
-    fc1_own = ordered(fc1_own, (D, hidden)).reshape(D, hidden)
-    fc1_other = swap(fc1_own, "k")
     down = jnp.concatenate(
         [w_fc2.reshape(LO, hidden, depth), w_out.reshape(LO, HD, depth)], axis=1
     )
@@ -930,16 +941,21 @@
     else:
         down_own = down.transpose(2, 1, 0, 3).reshape(hidden + HD, LO, 256).transpose(1, 0, 2)
     down_other = swap(down_own, "k")
+    fc2_own, fc2_other = down_own[:, :hidden], down_other[:, :hidden]
+    out2 = jnp.concatenate([down_own[:, hidden:], down_other[:, hidden:]], axis=1)
     if n_hi == 1:
         ids = half(position_ids, k)
         ids = jnp.stack([ids // BLK, ids % BLK]).astype(BF)
-        ids = jnp.concatenate([ids, jnp.zeros((IDS - 2, BLK), BF)])
-        heads_own = spread(pack_heads(w_qkv.transpose(1, 0, 2), ids))
-        qkv = join_heads(heads_own, swap(heads_own, "k"))
-        ids = heads_own[:, 3 * BLK : 3 * BLK + 2].astype(jnp.int32)
+        ids = jnp.pad(ids, ((0, IDS - 2), (0, BLK)))
+        first_own = spread(pack_first(w_fc1, w_qkv.transpose(1, 0, 2), ids))
+        fc1_own, fc1_other, qkv = join_first(first_own, swap(first_own, "k"))
+        ids = first_own[:, 3 * BLK + HALF : 3 * BLK + HALF + 2, :BLK].astype(jnp.int32)
         ids = ids[:, 0] * BLK + ids[:, 1]
         ids = jnp.stack([lax.dynamic_index_in_dim(ids, c, 0, keepdims=False) for c in slot_lo])
     else:
+        fc1_own = spread(over_hi(w_fc1).reshape(n_hi, depth, LO, hidden).transpose(2, 0, 1, 3))
+        fc1_own = ordered(fc1_own, (D, hidden)).reshape(D, hidden)
+        fc1_other = swap(fc1_own, "k")
         ids = half(position_ids, k)
         for name in ("zh", "zl", "x"):
             ids = jnp.stack([ids, swap(ids, name)])
@@ -1006,10 +1022,10 @@
 
     key_set = tuple(all_keys(v) for v in (keys, values, other_kv[0], other_kv[1]))
     attended, log_total = attend(tiles, blocks, table, queries, *key_set)
-    summed = scatter_pieces(*mix(place, attended, active, down_own, down_other))
+    summed = scatter_pieces(*mix(place, attended, active, out2, fc2_own, fc2_other))
 
     cot, grad_pre, grad_attended, term_bias1 = back(
-        place, pieces_cot, pre, down_own, down_other
+        place, pieces_cot, pre, out2, fc2_own, fc2_other
     )
 
     def summed_dot(left, own, other, flip):
@@ -1034,8 +1050,11 @@
     fc2_sum = add(*summed_dot(cot, active[:, :hidden], active[:, hidden:], True))
     out_sum = add(*summed_dot(cot, attended[:, :HD], attended[:, HD:], True))
     down = jnp.concatenate([cut_columns(fc2_sum), cut_columns(out_sum)], axis=2)
+    fc1_term, fc1_got = summed_dot(normed16, grad_pre[:, :hidden], grad_pre[:, hidden:], False)
     if n_hi == 1:
-        grad_attended, down = lax.optimization_barrier((grad_attended, down))
+        grad_attended, down, fc1_term, fc1_got = lax.optimization_barrier(
+            (grad_attended, down, fc1_term, fc1_got)
+        )
     down_home = home(down)
     grad_fc2 = down_home[:, :hidden].reshape(LO * hidden, depth).astype(F32)
     grad_out = down_home[:, hidden:].reshape(LO * HD, depth).astype(F32)
@@ -1057,17 +1076,10 @@
     joint, joint_own, joint_other, term_joint_bias = unturn(
         dq, dk, dv, got, cosine, sine_a, sine_b
     )
-    *partial, row_sums, gain_sum, shift_sum = grad_units(
-        place, pieces, mean, inv, gain, joint, grad_pre, qkv, fc1_own, fc1_other
-    )
-    if n_hi == 1:
-        late, *partial = lax.optimization_barrier((normed16, *partial))
-    else:
-        late = normed16
-    fc1_term, fc1_got = summed_dot(late, grad_pre[:, :hidden], grad_pre[:, hidden:], False)
-    own_term, got_term = summed_dot(late, joint_own, joint_other, False)
+    own_term, got_term = summed_dot(normed16, joint_own, joint_other, False)
     if n_hi == 1:
         packed = pack_grads(fc1_term, fc1_got, own_term, got_term)
+        packed, joint = lax.optimization_barrier((packed, joint))
         grad_fc1, grad_qkv = home_grads(spread(packed))
         grad_qkv = grad_qkv.transpose(1, 0, 2)
     else:
@@ -1077,6 +1089,9 @@
         qkv_sum = add(own_term, got_term).reshape(n_hi, LO, depth, 3 * HD)
         qkv_home = home(qkv_sum.transpose(1, 0, 2, 3)).reshape(LO, depth, 3, HD)
         grad_qkv = qkv_home.transpose(1, 2, 0, 3).reshape(depth, 3, width).astype(F32)
+    *partial, row_sums, gain_sum, shift_sum = grad_units(
+        place, pieces, mean, inv, gain, joint, grad_pre, qkv, fc1_own, fc1_other
+    )
     grad_unit = scatter_pieces(*partial)
 
     heads = lax.dynamic_update_slice(

time: 418 us -> 468 us (1.12)
  waiting for transfers between devices: 154 us -> 186 us
  matrix products: 23.3 us -> 30.2 us
  other arithmetic: 41.7 us -> 46.9 us
    all_to_all x5 -> x4, waiting for transfers between devices: 16.8 us -> 37.9 us  [spread(): return lax.all_to_all(pieces, LOX, 0, 0, tiled=True)]
    ppermute x48 -> x47, waiting for transfers between devices: 137 us -> 148 us  [swap(): return lax.ppermute(values, axis, [(0, 1), (1, 0)])]
    ppermute x48 -> x47, starting transfers between devices: 41.4 us -> 48.9 us  [swap(): return lax.ppermute(values, axis, [(0, 1), (1, 0)])]
    dot_general x8, matrix products: 23.3 us -> 30.2 us  [dot(): lax.dot_general(left, right, (((left_dim,), (right_dim,)), ((), ())), pre...]
    select_n x8, other arithmetic: 1.25 us -> 5.96 us  [in_order(): jnp.where(index == 0, jnp.concatenate([own, got], axis=axis), jnp.concate...]
    unnamed x154 -> x107, local copies, waits for them, and re-layouts: 11.8 us -> 7.37 us
    all_to_all x5 -> x4, starting transfers between devices: 23.5 us -> 19.7 us  [spread(): return lax.all_to_all(pieces, LOX, 0, 0, tiled=True)]
  transfers between devices with their start and end apart: 53 -> 51, of which waited for: 21 -> 19; matrix products, arithmetic and copies ran while one was open for 22% -> 23% of each run, Pallas kernels for 17% -> 15%
where the time goes in v2:
time: 468 us; the launch traced here: 459 us
  waiting for transfers between devices  186 us (40%)
  Pallas kernels  87.5 us (19%)
  starting transfers between devices  68.6 us (15%)
  other arithmetic  46.9 us (10%)
  local copies, waits for them, and re-layouts  38.3 us (8%)
  matrix products  30.2 us (6%)
    ppermute x47, waiting for transfers between devices, swap(): return lax.ppermute(values, axis, [(0, 1), (1, 0)])  148 us
    ppermute x47, starting transfers between devices, swap(): return lax.ppermute(values, axis, [(0, 1), (1, 0)])  48.9 us
    all_to_all x4, waiting for transfers between devices, spread(): return lax.all_to_all(pieces, LOX, 0, 0, tiled=True)  37.9 us
    dot_general x8, matrix products, dot(): lax.dot_general(left, right, (((left_dim,), (right_dim,)), ((), ())), pre...  30.2 us
    all_to_all x4, starting transfers between devices, spread(): return lax.all_to_all(pieces, LOX, 0, 0, tiled=True)  19.7 us
    pallas_call x1, Pallas kernels, front(): pl.pallas_call(front_kernel, grid=(tokens // STEP,), out_shape=(shape(D,...  13.6 us
    pallas_call x1, Pallas kernels, grad_units(): pl.pallas_call(grad_kernel, grid=(tokens // STEP,), out_shape=(*partial_s...  13.5 us
    pallas_call x1, Pallas kernels, attend_back(): pl.pallas_call(functools.partial(attend_back_kernel, tiles, blocks), out_...  12 us
  transfers between devices with their start and end apart: 51, of which 19 were waited for; matrix products, arithmetic and copies ran while one was open for 23% of the time, Pallas kernels for 15%

profile of v2, /device:TPU:0, one launch (start us, length us, event | category | flops | bytes accessed | tf_op | source)
XLA Modules:
  0.0 459.3 jit_solution(3253870580849381061)
XLA Ops:
  5.2 7.4 %all-to-all-start = ((bf16[8,464,256]{2,1,0:T(8,128)(2,1)}), bf16[8,464,256]{2,1,0:T(8,128)(2,1)S(1)}, u32[]{:S(2)}, u32[]{:S(2)}) async-start(bf16[8,464,256]{2,1,0:T(8,128)(2,1)} %pack.1), calls=%async_computation | async-start | bytes 3801088 | tf_op jit(solution)/shard_map/all_to_all | solution.py:38
  18.8 37.9 %all-to-all-done.own = bf16[8,464,256]{2,1,0:T(8,128)(2,1)S(1)} async-done(((bf16[8,464,256]{2,1,0:T(8,128)(2,1)}), bf16[8,464,256]{2,1,0:T(8,128)(2,1)S(1)}, u32[]{:S(2)}, u32[]{:S(2)}) %all-to-all-start) | async-done | bytes 1900576 | tf_op jit(solution)/shard_map/all_to_all | solution.py:38
  56.7 3.6 all-to-all-start.1
  70.3 32.9 %collective-permute-done.1 = bf16[2,64,1024]{2,1,0:T(8,128)(2,1)} collective-permute-done((bf16[2,64,1024]{2,1,0:T(8,128)(2,1)}, bf16[2,64,1024]{2,1,0:T(8,128)(2,1)}, u32[]{:S(2)}, u32[]{:S(2)}) %collective-permute-start.1) | collective-permute-done | bytes 262176 | tf_op jit(solution)/shard_map/ppermute | solution.py:34
  110.3 10.1 %collective-permute-done.22 = bf16[2,64,1024]{2,1,0:T(8,128)(2,1)S(1)} collective-permute-done((bf16[2,64,1024]{2,1,0:T(8,128)(2,1)S(1)}, bf16[2,64,1024]{2,1,0:T(8,128)(2,1)S(1)}, u32[]{:S(2)}, u32[]{:S(2)}) %collective-permute-start.22) | collective-permute-done | bytes 262176 | tf_op jit(solution)/shard_map/ppermute | solution.py:34
  121.3 4.0 collective-permute-start.23
  130.8 6.4 %collective-permute-done.23 = bf16[2,2,64,1024]{3,2,1,0:T(8,128)(2,1)} collective-permute-done((bf16[2,2,64,1024]{3,2,1,0:T(8,128)(2,1)}, bf16[2,2,64,1024]{3,2,1,0:T(8,128)(2,1)}, u32[]{:S(2)}, u32[]{:S(2)}) %collective-permute-start.23) | collective-permute-done | bytes 524320 | tf_op jit(solution)/shard_map/ppermute | solution.py:34
  147.5 6.6 %collective-permute-done.4.refs_2_ = bf16[4,64,1024]{2,1,0:T(8,128)(2,1)S(1)} collective-permute-done((bf16[4,64,1024]{2,1,0:T(8,128)(2,1)}, bf16[4,64,1024]{2,1,0:T(8,128)(2,1)S(1)}, u32[]{:S(2)}, u32[]{:S(2)}) %collective-permute-start.4) | collective-permute-done | bytes 524320 | tf_op jit(solution)/shard_map/ppermute | solution.py:34
  158.8 8.4 %collective-permute-done.24.refs_1_ = bf16[4,64,1024]{2,1,0:T(8,128)(2,1)} collective-permute-done((bf16[4,64,1024]{2,1,0:T(8,128)(2,1)}, bf16[4,64,1024]{2,1,0:T(8,128)(2,1)}, u32[]{:S(2)}, u32[]{:S(2)}) %collective-permute-start.24) | collective-permute-done | bytes 524320 | tf_op jit(solution)/shard_map/ppermute | solution.py:34
  170.7 9.7 %collective-permute-done.5.refs_3_ = bf16[4,64,1024]{2,1,0:T(8,128)(2,1)} collective-permute-done((bf16[4,64,1024]{2,1,0:T(8,128)(2,1)}, bf16[4,64,1024]{2,1,0:T(8,128)(2,1)}, u32[]{:S(2)}, u32[]{:S(2)}) %collective-permute-start.5) | collective-permute-done | bytes 524320 | tf_op jit(solution)/shard_map/ppermute | solution.py:34
  191.3 4.4 join.1
  195.7 13.6 %front.1 = (bf16[1024,2048]{1,0:T(8,128)(2,1)}, f32[1024,128]{1,0:T(8,128)}, f32[1024,128]{1,0:T(8,128)}, bf16[1024,128]{1,0:T(8,128)(2,1)}, bf16[1024,128]{1,0:...) custom-call(s32[10]{0:T(128)} %stack.124.place, ...), custom_call_target="tpu_custom_call" | custom-call | flops 3758096384 | bytes 12582912 | tf_op jit(solution)/shard_map/front/pallas_call | solution.py:566
  210.4 10.3 %back.1 = (bf16[1024,2048]{1,0:T(8,128)(2,1)}, bf16[1024,512]{1,0:T(8,128)(2,1)}, bf16[1024,128]{1,0:T(8,128)(2,1)}, f32[1,512]{1,0:T(1,128)}) custom-call(s32[10]{0:T(128)} %stack.124.place, bf16[4,64,1024]{2,1,0:T(8,128)(2,1)} %get-tuple-element.105.refs_0_, bf16[4,64,1024]{2,1,0:T(8,128)(2,1)} %collective-permute-done.24.refs_1_, ...), custom_call_target="tpu_custom_call" | custom-call | flops 2684354560 | bytes 14000000 | tf_op jit(solution)/shard_map/back/pallas_call | solution.py:738
  220.8 4.8 %convolution_convert_fusion = bf16[2048,256]{1,0:T(8,128)(2,1)} fusion(bf16[1024,2048]{1,0:T(8,128)(2,1)} %get-tuple-element.75, bf16[1024,512]{1,0:T(8,128)(2,1)} %get-tuple-element.76.refs_12_), kind=kOutput, calls=%fused_computation.2 | convolution fusion | flops 1074266112 | bytes 5767168 | tf_op jit(solution)/shard_map/dot_general | solution.py:73
  229.5 4.8 %fusion.21.fc1_own = f32[2048,256]{1,0:T(8,128)} fusion(bf16[1024,2048]{1,0:T(8,128)(2,1)} %get-tuple-element.75, bf16[1024,512]{1,0:T(8,128)(2,1)S(1)} %copy-done.42), kind=kOutput, calls=%fused_computation.69 | convolution fusion | flops 1073741824 | bytes 6815744 | tf_op jit(solution)/shard_map/dot_general | solution.py:73
  235.2 9.9 %attend.1 = (bf16[1024,128]{1,0:T(8,128)(2,1)}, f32[1024,128]{1,0:T(8,128)}) custom-call(s32[49]{0:T(128)} %pad_add_fusion.table, bf16[1024,128]{1,0:T(8,128)(2,1)} %get-tuple-element.60.q, bf16[1024,128]{1,0:T(8,128)(2,1)} %get-tuple-element.61.k_own, bf16[1024,128]{1,0:T(8,128)(2,1)} %get-tuple-element.62.v_own, ...), custom_call_target="tpu_custom_call" | custom-call | flops 2684354560 | bytes 2000000 | tf_op jit(solution)/shard_map/attend/pallas_call | solution.py:338
  248.9 8.3 %mix.1 = (bf16[8,64,1024]{2,1,0:T(8,128)(2,1)}, bf16[8,64,1024]{2,1,0:T(8,128)(2,1)}, bf16[4,2,64,1024]{3,2,1,0:T(8,128)(2,1)}, bf16[4,2,64,1024]{3,2,1,0:T(8,128)(2,1)}) custom-call(s32[10]{0:T(128)} %stack.124.place, bf16[1024,128]{1,0:T(8,128)(2,1)} %get-tuple-element.64.attended.att, bf16[1024,512]{1,0:T(8,128)(2,1)} %get-tuple-element.65.active, ...), custom_call_target="tpu_custom_call" | custom-call | flops 2684354560 | bytes 8000000 | tf_op jit(solution)/shard_map/mix/pallas_call | solution.py:672
  258.7 3.5 fusion.1
  266.6 12.0 %attend_back.1 = (f32[1024,128]{1,0:T(8,128)}, f32[1024,128]{1,0:T(8,128)}, f32[1024,128]{1,0:T(8,128)}, bf16[2,1024,128]{2,1,0:T(8,128)(2,1)}) custom-call(s32[49]{0:T(128)} %pad_add_fusion.table, bf16[1024,128]{1,0:T(8,128)(2,1)} %get-tuple-element.60.q, bf16[1024,128]{1,0:T(8,128)(2,1)} %get-tuple-element.61.k_own, ...), custom_call_target="tpu_custom_call" | custom-call | flops 6710886400 | bytes 6000000 | tf_op jit(solution)/shard_map/attend_back/pallas_call | solution.py:470
  280.5 3.8 all-to-all-start.3
  284.3 4.2 unturn.1
  288.5 4.2 convolution_convert_fusion.2
  302.5 4.8 %fusion.61.own = f32[2048,192]{1,0:T(8,128)} fusion(bf16[1024,2048]{1,0:T(8,128)(2,1)} %get-tuple-element.75, bf16[1024,192]{1,0:T(8,128)(2,1)S(1)} %copy-done.41), kind=kOutput, calls=%fused_computation.205 | convolution fusion | flops 805306368 | bytes 6160384 | tf_op jit(solution)/shard_map/dot_general | solution.py:73
  309.5 4.5 pack_grad.1
  314.0 13.5 %grad.1 = (bf16[8,64,1024]{2,1,0:T(8,128)(2,1)}, bf16[8,64,1024]{2,1,0:T(8,128)(2,1)}, bf16[4,2,64,1024]{3,2,1,0:T(8,128)(2,1)}, bf16[4,2,64,1024]{3,2,1,0:T(8,1...) custom-call(s32[10]{0:T(128)} %stack.124.place, ...), custom_call_target="tpu_custom_call" | custom-call | flops 3758096384 | bytes 16000000 | tf_op jit(solution)/shard_map/grad/pallas_call | solution.py:850
  340.3 4.7 %collective-permute-done.17 = bf16[4,64,1024]{2,1,0:T(8,128)(2,1)} collective-permute-done((bf16[4,64,1024]{2,1,0:T(8,128)(2,1)S(1)}, bf16[4,64,1024]{2,1,0:T(8,128)(2,1)}, u32[]{:S(2)}, u32[]{:S(2)}) %collective-permute-start.17) | collective-permute-done | bytes 524320 | tf_op jit(solution)/shard_map/ppermute | solution.py:34
  354.0 16.5 %collective-permute-done.35 = bf16[8,64,1024]{2,1,0:T(8,128)(2,1)} collective-permute-done((bf16[8,64,1024]{2,1,0:T(8,128)(2,1)}, bf16[8,64,1024]{2,1,0:T(8,128)(2,1)}, u32[]{:S(2)}, u32[]{:S(2)}) %collective-permute-start.35) | collective-permute-done | bytes 1048608 | tf_op jit(solution)/shard_map/ppermute | solution.py:34
  379.8 4.4 collective-permute-done.36
  385.3 4.8 %all-to-all-start.2 = ((bf16[8,448,256]{2,1,0:T(8,128)(2,1)}), bf16[8,448,256]{2,1,0:T(8,128)(2,1)S(1)}, u32[]{:S(2)}, u32[]{:S(2)}) async-start(bf16[8,448,256]{2,1,0:T(8,128)(2,1)} %pack_grad.1), calls=%async_computation.2 | async-start | bytes 3670016 | tf_op jit(solution)/shard_map/all_to_all | solution.py:38
  402.3 28.8 %collective-permute-done.39 = bf16[2,2,64,1024]{3,2,0,1:T(8,128)(2,1)} collective-permute-done((bf16[2,2,64,1024]{3,2,0,1:T(8,128)(2,1)}, bf16[2,2,64,1024]{3,2,0,1:T(8,128)(2,1)}, u32[]{:S(2)}, u32[]{:S(2)}) %collective-permute-start.39) | collective-permute-done | bytes 524320 | tf_op jit(solution)/shard_map/ppermute | solution.py:34
  436.5 8.8 %collective-permute-done.40 = bf16[2,64,1024]{2,1,0:T(8,128)(2,1)S(1)} collective-permute-done((bf16[2,64,1024]{2,1,0:T(8,128)(2,1)S(1)}, bf16[2,64,1024]{2,1,0:T(8,128)(2,1)S(1)}, u32[]{:S(2)}, u32[]{:S(2)}) %collective-permute-start.40) | collective-permute-done | bytes 262176 | tf_op jit(solution)/shard_map/ppermute | solution.py:34
  454.7 3.7 home.1
  (338 shorter events, 151.9 us)
Async XLA Ops:
  5.2 51.5 %all-to-all-start = ((bf16[8,464,256]{2,1,0:T(8,128)(2,1)}), bf16[8,464,256]{2,1,0:T(8,128)(2,1)S(1)}, u32[]{:S(2)}, u32[]{:S(2)}) async-start(bf16[8,464,256]{2,1,0:T(8,128)(2,1)} %pack.1), calls=%async_computation | async-start | bytes 3801088 | tf_op jit(solution)/shard_map/all_to_all | solution.py:38
  13.3 48.3 %collective-permute-start = (bf16[128,512]{1,0:T(8,128)(2,1)}, bf16[128,512]{1,0:T(8,128)(2,1)}, u32[]{:S(2)}, u32[]{:S(2)}) collective-permute-start(bf16[128,512]{1,0:T(8,128)(2,1)} %bitcast.12), channel_id=1, source_target_pairs={{0,1},{1,0},{2,3},{3,2},{4,5},{5,4},{6,7},{7,6},{8,9},{9,8},{10,11... | collective-permute-start | bytes 393224 | tf_op jit(solution)/shard_map/ppermute | solution.py:34
  14.4 53.2 %collective-permute-start.9 = (f32[1472]{0:T(1024)S(1)}, f32[1472]{0:T(1024)S(1)}, u32[]{:S(2)}, u32[]{:S(2)}) collective-permute-start(f32[1472]{0:T(1024)S(1)} %concatenate.174), channel_id=1, source_target_pairs={{0,1},{1,0},{2,3},{3,2},{4,5},{5,4},{6,7},{7,6},{8,9},{9,8},{10,11... | collective-permute-start | bytes 17672 | tf_op jit(solution)/shard_map/ppermute | solution.py:34
  16.5 87.8 %collective-permute-start.21 = (bf16[128,512]{1,0:T(8,128)(2,1)}, bf16[128,512]{1,0:T(8,128)(2,1)}, u32[]{:S(2)}, u32[]{:S(2)}) collective-permute-start(bf16[128,512]{1,0:T(8,128)(2,1)} %bitcast.48), channel_id=1, source_target_pairs={{0,1},{1,0},{2,3},{3,2},{4,5},{5,4},{6,7},{7,6},{8,9},{9,8},{10,11... | collective-permute-start | bytes 393224 | tf_op jit(solution)/shard_map/ppermute | solution.py:34
  56.7 73.5 %all-to-all-start.1 = ((bf16[8,1,320,256]{3,2,1,0:T(8,128)(2,1)}), bf16[8,1,320,256]{3,2,1,0:T(8,128)(2,1)S(1)}, u32[]{:S(2)}, u32[]{:S(2)}) async-start(bf16[8,1,320,256]{3,2,1,0:T(8,128)(2,1)} %maximum_bitcast_fusion), calls=%async_computation.1 | async-start | bytes 2621440 | tf_op jit(solution)/shard_map/all_to_all | solution.py:38
  63.4 39.8 %collective-permute-start.1 = (bf16[2,64,1024]{2,1,0:T(8,128)(2,1)}, bf16[2,64,1024]{2,1,0:T(8,128)(2,1)}, u32[]{:S(2)}, u32[]{:S(2)}) collective-permute-start(bf16[2,64,1024]{2,1,0:T(8,128)(2,1)} %maximum_select_fusion.3), channel_id=1, source_target_pairs={{0,16},{16,0},{1,17},{17,1},{2,18},{18,2},{3,19},{19,3},{4,20},{20... | collective-permute-start | bytes 786440 | tf_op jit(solution)/shard_map/ppermute | solution.py:34
  67.6 60.9 %collective-permute-start.10 = (f32[2,1024]{1,0:T(2,128)S(1)}, f32[2,1024]{1,0:T(2,128)S(1)}, u32[]{:S(2)}, u32[]{:S(2)}) collective-permute-start(f32[2,1024]{1,0:T(2,128)S(1)} %maximum_select_fusion.9), channel_id=1, source_target_pairs={{0,2},{2,0},{1,3},{3,1},{4,6},{6,4},{5,7},{7,5},{8,10},{10,8},{9,1... | collective-permute-start | bytes 24584 | tf_op jit(solution)/shard_map/ppermute | solution.py:34
  104.2 21.1 %collective-permute-start.2 = (bf16[2,2,64,1024]{3,2,0,1:T(8,128)(2,1)S(1)}, bf16[2,2,64,1024]{3,2,0,1:T(8,128)(2,1)S(1)}, u32[]{:S(2)}, u32[]{:S(2)}) collective-permute-start(bf16[2,2,64,1024]{3,2,0,1:T(8,128)(2,1)S(1)} %pad_maximum_fusion.5), channel_id=1, source_target_pairs={{0,8},{8,0},{1,9},{9,1},{2,10},{10,2},{3,11},{11,3},{4,12},{12,4},... | collective-permute-start | bytes 1572872 | tf_op jit(solution)/shard_map/ppermute | solution.py:34
  126.4 56.6 %collective-permute-start.11 = (bf16[8,464,256]{2,1,0:T(8,128)(2,1)S(1)}, bf16[8,464,256]{2,1,0:T(8,128)(2,1)}, u32[]{:S(2)}, u32[]{:S(2)}) collective-permute-start(bf16[8,464,256]{2,1,0:T(8,128)(2,1)S(1)} %all-to-all-done.own), channel_id=1, source_target_pairs={{0,1},{1,0},{2,3},{3,2},{4,5},{5,4},{6,7},{7,6},{8,9},{9,8},{10,11... | collective-permute-start | bytes 5701640 | tf_op jit(solution)/shard_map/ppermute | solution.py:34
  128.6 18.0 %collective-permute-start.7 = (bf16[4,64,1024]{2,1,0:T(8,128)(2,1)}, bf16[4,64,1024]{2,1,0:T(8,128)(2,1)}, u32[]{:S(2)}, u32[]{:S(2)}) collective-permute-start(bf16[4,64,1024]{2,1,0:T(8,128)(2,1)} %get-tuple-element.106.refs_4_), channel_id=1, source_target_pairs={{0,2},{2,0},{1,3},{3,1},{4,6},{6,4},{5,7},{7,5},{8,10},{10,8},{9,1... | collective-permute-start | bytes 1572872 | tf_op jit(solution)/shard_map/ppermute | solution.py:34
  130.1 51.3 %collective-permute-start.13 = (bf16[8,320,256]{2,1,0:T(8,128)(2,1)S(1)}, bf16[8,320,256]{2,1,0:T(8,128)(2,1)}, u32[]{:S(2)}, u32[]{:S(2)}) collective-permute-start(bf16[8,320,256]{2,1,0:T(8,128)(2,1)S(1)} %bitcast.223), channel_id=1, source_target_pairs={{0,1},{1,0},{2,3},{3,2},{4,5},{5,4},{6,7},{7,6},{8,9},{9,8},{10,11... | collective-permute-start | bytes 3932168 | tf_op jit(solution)/shard_map/ppermute | solution.py:34
  137.2 16.9 %collective-permute-start.4 = (bf16[4,64,1024]{2,1,0:T(8,128)(2,1)}, bf16[4,64,1024]{2,1,0:T(8,128)(2,1)S(1)}, u32[]{:S(2)}, u32[]{:S(2)}) collective-permute-start(bf16[4,64,1024]{2,1,0:T(8,128)(2,1)} %get-tuple-element.107.refs_0_), channel_id=1, source_target_pairs={{0,2},{2,0},{1,3},{3,1},{4,6},{6,4},{5,7},{7,5},{8,10},{10,8},{9,1... | collective-permute-start | bytes 1572872 | tf_op jit(solution)/shard_map/ppermute | solution.py:34
  146.5 20.6 %collective-permute-start.24 = (bf16[4,64,1024]{2,1,0:T(8,128)(2,1)}, bf16[4,64,1024]{2,1,0:T(8,128)(2,1)}, u32[]{:S(2)}, u32[]{:S(2)}) collective-permute-start(bf16[4,64,1024]{2,1,0:T(8,128)(2,1)} %get-tuple-element.105.refs_0_), channel_id=1, source_target_pairs={{0,4},{4,0},{1,5},{5,1},{2,6},{6,2},{3,7},{7,3},{8,12},{12,8},{9,1... | collective-permute-start | bytes 1572872 | tf_op jit(solution)/shard_map/ppermute | solution.py:34
  157.2 23.3 %collective-permute-start.5 = (bf16[4,64,1024]{2,1,0:T(8,128)(2,1)}, bf16[4,64,1024]{2,1,0:T(8,128)(2,1)}, u32[]{:S(2)}, u32[]{:S(2)}) collective-permute-start(bf16[4,64,1024]{2,1,0:T(8,128)(2,1)} %collective-permute-done.3.refs_1_), channel_id=1, source_target_pairs={{0,2},{2,0},{1,3},{3,1},{4,6},{6,4},{5,7},{7,5},{8,10},{10,8},{9,1... | collective-permute-start | bytes 1572872 | tf_op jit(solution)/shard_map/ppermute | solution.py:34
  167.2 28.6 %collective-permute-start.8 = (bf16[4,64,1024]{2,1,0:T(8,128)(2,1)}, bf16[4,64,1024]{2,1,0:T(8,128)(2,1)}, u32[]{:S(2)}, u32[]{:S(2)}) collective-permute-start(bf16[4,64,1024]{2,1,0:T(8,128)(2,1)} %collective-permute-done.7.refs_6_), channel_id=1, source_target_pairs={{0,4},{4,0},{1,5},{5,1},{2,6},{6,2},{3,7},{7,3},{8,12},{12,8},{9,1... | collective-permute-start | bytes 1572872 | tf_op jit(solution)/shard_map/ppermute | solution.py:34
  169.2 40.1 %collective-permute-start.25 = (bf16[4,64,1024]{2,1,0:T(8,128)(2,1)}, bf16[4,64,1024]{2,1,0:T(8,128)(2,1)}, u32[]{:S(2)}, u32[]{:S(2)}) collective-permute-start(bf16[4,64,1024]{2,1,0:T(8,128)(2,1)} %get-tuple-element.105.refs_0_), channel_id=1, source_target_pairs={{0,2},{2,0},{1,3},{3,1},{4,6},{6,4},{5,7},{7,5},{8,10},{10,8},{9,1... | collective-permute-start | bytes 1572872 | tf_op jit(solution)/shard_map/ppermute | solution.py:34
  180.5 28.9 %collective-permute-start.27 = (bf16[4,64,1024]{2,1,0:T(8,128)(2,1)}, bf16[4,64,1024]{2,1,0:T(8,128)(2,1)}, u32[]{:S(2)}, u32[]{:S(2)}) collective-permute-start(bf16[4,64,1024]{2,1,0:T(8,128)(2,1)} %get-tuple-element.104.refs_4_), channel_id=1, source_target_pairs={{0,4},{4,0},{1,5},{5,1},{2,6},{6,2},{3,7},{7,3},{8,12},{12,8},{9,1... | collective-permute-start | bytes 1572872 | tf_op jit(solution)/shard_map/ppermute | solution.py:34
  181.5 27.9 %collective-permute-start.26 = (bf16[4,64,1024]{2,1,0:T(8,128)(2,1)}, bf16[4,64,1024]{2,1,0:T(8,128)(2,1)S(1)}, u32[]{:S(2)}, u32[]{:S(2)}) collective-permute-start(bf16[4,64,1024]{2,1,0:T(8,128)(2,1)} %collective-permute-done.24.refs_1_), channel_id=1, source_target_pairs={{0,2},{2,0},{1,3},{3,1},{4,6},{6,4},{5,7},{7,5},{8,10},{10,8},{9,1... | collective-permute-start | bytes 1572872 | tf_op jit(solution)/shard_map/ppermute | solution.py:34
  183.0 26.4 %collective-permute-start.29 = (bf16[4,64,1024]{2,1,0:T(8,128)(2,1)}, bf16[4,64,1024]{2,1,0:T(8,128)(2,1)S(1)}, u32[]{:S(2)}, u32[]{:S(2)}) collective-permute-start(bf16[4,64,1024]{2,1,0:T(8,128)(2,1)} %collective-permute-done.28.refs_6_), channel_id=1, source_target_pairs={{0,4},{4,0},{1,5},{5,1},{2,6},{6,2},{3,7},{7,3},{8,12},{12,8},{9,1... | collective-permute-start | bytes 1572872 | tf_op jit(solution)/shard_map/ppermute | solution.py:34
  225.5 41.1 %collective-permute-start.32 = (bf16[2048,256]{1,0:T(8,128)(2,1)}, bf16[2048,256]{1,0:T(8,128)(2,1)}, u32[]{:S(2)}, u32[]{:S(2)}) collective-permute-start(bf16[2048,256]{1,0:T(8,128)(2,1)} %convolution_convert_fusion), channel_id=1, source_target_pairs={{0,1},{1,0},{2,3},{3,2},{4,5},{5,4},{6,7},{7,6},{8,9},{9,8},{10,11... | collective-permute-start | bytes 3145736 | tf_op jit(solution)/shard_map/ppermute | solution.py:34
  228.3 34.0 %collective-permute-start.30 = (bf16[256,2048]{1,0:T(8,128)(2,1)}, bf16[256,2048]{1,0:T(8,128)(2,1)}, u32[]{:S(2)}, u32[]{:S(2)}) collective-permute-start(bf16[256,2048]{1,0:T(8,128)(2,1)} %convolution_convert_fusion.1), channel_id=1, source_target_pairs={{0,1},{1,0},{2,3},{3,2},{4,5},{5,4},{6,7},{7,6},{8,9},{9,8},{10,11... | collective-permute-start | bytes 3145736 | tf_op jit(solution)/shard_map/ppermute | solution.py:34
  257.1 36.4 %collective-permute-start.14 = (bf16[8,64,1024]{2,1,0:T(8,128)(2,1)}, bf16[8,64,1024]{2,1,0:T(8,128)(2,1)S(1)}, u32[]{:S(2)}, u32[]{:S(2)}) collective-permute-start(bf16[8,64,1024]{2,1,0:T(8,128)(2,1)} %get-tuple-element.67), channel_id=1, source_target_pairs={{0,2},{2,0},{1,3},{3,1},{4,6},{6,4},{5,7},{7,5},{8,10},{10,8},{9,1... | collective-permute-start | bytes 3145736 | tf_op jit(solution)/shard_map/ppermute | solution.py:34
  257.7 41.8 %collective-permute-start.16 = (bf16[4,2,64,1024]{3,2,1,0:T(8,128)(2,1)}, bf16[4,2,64,1024]{3,2,1,0:T(8,128)(2,1)S(1)}, u32[]{:S(2)}, u32[]{:S(2)}) collective-permute-start(bf16[4,2,64,1024]{3,2,1,0:T(8,128)(2,1)} %get-tuple-element.69), channel_id=1, source_target_pairs={{0,4},{4,0},{1,5},{5,1},{2,6},{6,2},{3,7},{7,3},{8,12},{12,8},{9,1... | collective-permute-start | bytes 3145736 | tf_op jit(solution)/shard_map/ppermute | solution.py:34
  280.5 104.8 %all-to-all-start.3 = ((bf16[8,1,320,256]{3,2,1,0:T(8,128)(2,1)}), bf16[8,1,320,256]{3,2,1,0:T(8,128)(2,1)S(1)}, u32[]{:S(2)}, u32[]{:S(2)}) async-start(bf16[8,1,320,256]{3,2,1,0:T(8,128)(2,1)} %pad_maximum_fusion), calls=%async_computation.3 | async-start | bytes 2621440 | tf_op jit(solution)/shard_map/all_to_all | solution.py:38
  297.4 37.5 %collective-permute-start.15 = (bf16[4,64,1024]{2,1,0:T(8,128)(2,1)}, bf16[4,64,1024]{2,1,0:T(8,128)(2,1)}, u32[]{:S(2)}, u32[]{:S(2)}) collective-permute-start(bf16[4,64,1024]{2,1,0:T(8,128)(2,1)} %slice.385), channel_id=1, source_target_pairs={{0,4},{4,0},{1,5},{5,1},{2,6},{6,2},{3,7},{7,3},{8,12},{12,8},{9,1... | collective-permute-start | bytes 1572872 | tf_op jit(solution)/shard_map/ppermute | solution.py:34
  346.3 24.3 %collective-permute-start.35 = (bf16[8,64,1024]{2,1,0:T(8,128)(2,1)}, bf16[8,64,1024]{2,1,0:T(8,128)(2,1)}, u32[]{:S(2)}, u32[]{:S(2)}) collective-permute-start(bf16[8,64,1024]{2,1,0:T(8,128)(2,1)} %get-tuple-element.90), channel_id=1, source_target_pairs={{0,2},{2,0},{1,3},{3,1},{4,6},{6,4},{5,7},{7,5},{8,10},{10,8},{9,1... | collective-permute-start | bytes 3145736 | tf_op jit(solution)/shard_map/ppermute | solution.py:34
  347.0 26.0 %collective-permute-start.37 = (bf16[4,2,64,1024]{3,2,1,0:T(8,128)(2,1)}, bf16[4,2,64,1024]{3,2,1,0:T(8,128)(2,1)}, u32[]{:S(2)}, u32[]{:S(2)}) collective-permute-start(bf16[4,2,64,1024]{3,2,1,0:T(8,128)(2,1)} %get-tuple-element.92), channel_id=1, source_target_pairs={{0,4},{4,0},{1,5},{5,1},{2,6},{6,2},{3,7},{7,3},{8,12},{12,8},{9,1... | collective-permute-start | bytes 3145736 | tf_op jit(solution)/shard_map/ppermute | solution.py:34
  350.6 25.6 %collective-permute-start.18 = (bf16[2,2,64,1024]{3,2,0,1:T(8,128)(2,1)}, bf16[2,2,64,1024]{3,2,0,1:T(8,128)(2,1)}, u32[]{:S(2)}, u32[]{:S(2)}) collective-permute-start(bf16[2,2,64,1024]{3,2,0,1:T(8,128)(2,1)} %pad_maximum_fusion.4), channel_id=1, source_target_pairs={{0,8},{8,0},{1,9},{9,1},{2,10},{10,2},{3,11},{11,3},{4,12},{12,4},... | collective-permute-start | bytes 1572872 | tf_op jit(solution)/shard_map/ppermute | solution.py:34
  377.5 18.7 %collective-permute-start.19 = (bf16[2,64,1024]{2,1,0:T(8,128)(2,1)S(1)}, bf16[2,64,1024]{2,1,0:T(8,128)(2,1)}, u32[]{:S(2)}, u32[]{:S(2)}) collective-permute-start(bf16[2,64,1024]{2,1,0:T(8,128)(2,1)S(1)} %slice_bitcast_fusion.10), channel_id=1, source_target_pairs={{0,16},{16,0},{1,17},{17,1},{2,18},{18,2},{3,19},{19,3},{4,20},{20... | collective-permute-start | bytes 786440 | tf_op jit(solution)/shard_map/ppermute | solution.py:34
  385.3 68.3 %all-to-all-start.2 = ((bf16[8,448,256]{2,1,0:T(8,128)(2,1)}), bf16[8,448,256]{2,1,0:T(8,128)(2,1)S(1)}, u32[]{:S(2)}, u32[]{:S(2)}) async-start(bf16[8,448,256]{2,1,0:T(8,128)(2,1)} %pack_grad.1), calls=%async_computation.2 | async-start | bytes 3670016 | tf_op jit(solution)/shard_map/all_to_all | solution.py:38
  394.2 37.0 %collective-permute-start.39 = (bf16[2,2,64,1024]{3,2,0,1:T(8,128)(2,1)}, bf16[2,2,64,1024]{3,2,0,1:T(8,128)(2,1)}, u32[]{:S(2)}, u32[]{:S(2)}) collective-permute-start(bf16[2,2,64,1024]{3,2,0,1:T(8,128)(2,1)} %pad_maximum_fusion.3), channel_id=1, source_target_pairs={{0,8},{8,0},{1,9},{9,1},{2,10},{10,2},{3,11},{11,3},{4,12},{12,4},... | collective-permute-start | bytes 1572872 | tf_op jit(solution)/shard_map/ppermute | solution.py:34
  402.2 32.3 %collective-permute-start.20 = (f32[128,512]{1,0:T(8,128)S(1)}, f32[128,512]{1,0:T(8,128)S(1)}, u32[]{:S(2)}, u32[]{:S(2)}) collective-permute-start(f32[128,512]{1,0:T(8,128)S(1)} %bitcast.248), channel_id=1, source_target_pairs={{0,1},{1,0},{2,3},{3,2},{4,5},{5,4},{6,7},{7,6},{8,9},{9,8},{10,11... | collective-permute-start | bytes 786440 | tf_op jit(solution)/shard_map/ppermute | solution.py:34
  (64 other events, 925.2 us)
